TPU v7x, 128 devices: a whole 4x4x4 slice. The times are simulated.
128 devices in a mesh: group: 8 (over y, x_lo), tensor: 16 (over x_hi, z, core).
Axes of the slice: x: 4 (x_hi: 2, x_lo: 2; x = x_hi * 2 + x_lo), y: 4, z: 4, core: 2. Of those that a mesh axis runs over, the one named last changes fastest.
Arguments:
- prefill_states: bfloat16 [32768, 8192], P('group', 'tensor'), may hold values from -6 to 6
- key_weight: bfloat16 [8192, 1024], P('tensor'), may hold values from -0.0625 to 0.0625
- value_weight: bfloat16 [8192, 1024], P('tensor'), may hold values from -0.0625 to 0.0625
- page_slot: int32 [8, 16, 32], P('group', 'tensor'), may hold values from 0 to 31, each once within a row
- decode_states: bfloat16 [32, 8192], P('group'), may hold values from -6 to 6
- query_weight: bfloat16 [8192, 8192], P(None, 'tensor'), may hold values from -0.0625 to 0.0625
- cache_keys: bfloat16 [32, 8192, 1024], P('group', 'tensor'), may hold values from -606 to 606
- cache_values: bfloat16 [32, 8192, 1024], P('group', 'tensor'), may hold values from -6 to 6
- cached_length: int32 [32], P('group'), may hold values from 1 to 8192
Outputs:
- attention_out: bfloat16 [32, 8192], P('group', 'tensor')
Inputs may be any that keep to these rules, and one draw needn't show every extreme that they name: For every group g and block t, page_slot[g, t, :] is a permutation of 0 to 31.
All inputs are finite; a program needn't handle non-finite values.
Results may differ from a plain program's by a relative error of at most 0.017.
Values may be sent and summed in bfloat16 or wider, within the bound.
No kernel may reach another device: no remote copies, remote signals or barrier semaphores. Data moves between devices by JAX's collectives and lax.ppermute only.
A program may use at most 192 MiB of HBM per device.

v0:
```python
import jax
import jax.numpy as jnp
from jax import lax
from jax.sharding import PartitionSpec as P

HEAD_WIDTH = 128
PAGE = 8


rope_theta = 500000.0
masked_score = -1e30


def in_one_piece(arrays, axis, dim, along):
    both = jnp.concatenate(arrays, axis=along)
    whole, at, gathered = (lax.all_gather(both, axis, axis=dim, tiled=True), 0, [])
    for a in arrays:
        gathered.append(lax.slice_in_dim(whole, at, at + a.shape[along], axis=along))
        at += a.shape[along]
    return tuple(gathered)


def side_by_side(arrays, axis, split_dim, concat_dim, along):
    widths = [a.shape[along] for a in arrays]
    both = jnp.concatenate(arrays, axis=along)
    whole = lax.all_to_all(both, axis, split_axis=split_dim, concat_axis=concat_dim, tiled=True)
    return tuple(jnp.split(whole, [sum(widths[:k]) for k in range(1, len(widths))], axis=along))


def sent_to_all(array, axis):
    devices = lax.axis_size(axis)
    return lax.all_to_all(
        jnp.broadcast_to(array[None], (devices, *array.shape)), axis, 0, 0, tiled=True
    )


def laid_out(pieces, dim):
    shape = list(pieces.shape[1:])
    shape[dim] *= pieces.shape[0]
    return jnp.moveaxis(pieces, 0, dim).reshape(shape)


def gather_directly(array, axis, dim):
    pieces = sent_to_all(array, axis)
    return laid_out(pieces, dim)


def in_one_piece_2(arrays, axis, split_dim, concat_dim, along):
    columns = [a.reshape(*a.shape[:along], -1) for a in arrays]
    both = jnp.concatenate(columns, axis=along)
    whole, at, gathered = (
        lax.all_to_all(both, axis, split_axis=split_dim, concat_axis=concat_dim, tiled=True),
        0,
        [],
    )
    for a, column in zip(arrays, columns):
        slab = whole[..., at : at + column.shape[along]]
        gathered.append(slab.reshape(*slab.shape[:along], *a.shape[along:]))
        at += column.shape[along]
    return tuple(gathered)


def apply_rotary(vectors, positions):
    half_width = vectors.shape[-1] // 2
    index_float = jnp.arange(half_width, dtype=jnp.float32)
    frequency = rope_theta ** (-2.0 * index_float / vectors.shape[-1])
    angles = positions[..., None].astype(jnp.float32) * frequency
    cosine_part = jnp.cos(angles)
    sine_part = jnp.sin(angles)
    first_half = vectors[..., :half_width]
    second_half = vectors[..., half_width:]
    return jnp.concatenate(
        [
            first_half * cosine_part - second_half * sine_part,
            second_half * cosine_part + first_half * sine_part,
        ],
        axis=-1,
    )


def per_device(
    prefill_states,
    key_weight,
    value_weight,
    page_slot,
    decode_states,
    query_weight,
    cache_keys,
    cache_values,
    cached_length,
):
    tensor_size = lax.axis_size("tensor")
    tensor_rank = lax.axis_index("tensor")
    rows_total = prefill_states.shape[0]
    fresh_count = rows_total // tensor_size
    kv_width = key_weight.shape[1]
    kv_heads = kv_width // HEAD_WIDTH
    token_block = lax.all_to_all(prefill_states, "tensor", split_axis=0, concat_axis=1, tiled=True)
    pieces = in_one_piece((key_weight, value_weight), "tensor", 0, 1)
    fresh_keys = jnp.dot(token_block, pieces[0], preferred_element_type=jnp.float32)
    fresh_values = jnp.dot(token_block, pieces[1], preferred_element_type=jnp.float32)
    fresh_keys = fresh_keys.astype(jnp.bfloat16)
    fresh_values = fresh_values.astype(jnp.bfloat16)
    page_count = fresh_count // PAGE
    slot_order = page_slot.reshape(page_count)
    picker = (slot_order[None, :] == jnp.arange(page_count, dtype=jnp.int32)[:, None]).astype(
        jnp.bfloat16
    )
    sorted_keys = jnp.dot(
        picker, fresh_keys.reshape(page_count, PAGE * kv_width), preferred_element_type=jnp.float32
    ).astype(jnp.bfloat16)
    sorted_values = jnp.dot(
        picker,
        fresh_values.reshape(page_count, PAGE * kv_width),
        preferred_element_type=jnp.float32,
    ).astype(jnp.bfloat16)
    moved_keys, moved_values = side_by_side((sorted_keys, sorted_values), "group", 0, 0, 1)
    decode_rows = decode_states.shape[0]
    fresh_per_row = fresh_count // decode_rows
    fresh_position_index = (
        cached_length[:, None]
        + tensor_rank * fresh_per_row
        + jnp.arange(fresh_per_row, dtype=jnp.int32)[None, :]
    )
    placed = moved_keys.reshape(decode_rows, fresh_per_row, kv_heads, HEAD_WIDTH).astype(
        jnp.float32
    )
    incoming_keys = apply_rotary(placed, fresh_position_index[:, :, None]).astype(jnp.bfloat16)
    incoming_values = moved_values.reshape(decode_rows, fresh_per_row, kv_heads, HEAD_WIDTH)
    local_queries = jnp.dot(decode_states, query_weight, preferred_element_type=jnp.float32)
    local_heads = local_queries.shape[1] // HEAD_WIDTH
    query_position = cached_length + tensor_size * fresh_per_row
    local_queries = (
        apply_rotary(
            local_queries.reshape(decode_rows, local_heads, HEAD_WIDTH), query_position[:, None]
        )
        .reshape(decode_rows, local_heads * HEAD_WIDTH)
        .astype(jnp.bfloat16)
    )
    query_vectors = gather_directly(local_queries, "tensor", 1)
    head_total = query_vectors.shape[1] // HEAD_WIDTH
    group_size = head_total // kv_heads
    grouped = query_vectors.reshape(decode_rows, kv_heads, group_size, HEAD_WIDTH)
    context_dev = cache_keys.shape[1]
    prior_keys = cache_keys.reshape(decode_rows, context_dev, kv_heads, HEAD_WIDTH)
    prior_values = cache_values.reshape(decode_rows, context_dev, kv_heads, HEAD_WIDTH)
    inv_scale = 1.0 / HEAD_WIDTH**0.5
    old_scores = (
        jnp.einsum("bhgd,blhd->bhgl", grouped, prior_keys, preferred_element_type=jnp.float32)
        * inv_scale
    )
    new_scores = (
        jnp.einsum("bhgd,blhd->bhgl", grouped, incoming_keys, preferred_element_type=jnp.float32)
        * inv_scale
    )
    usable = (tensor_rank * context_dev + jnp.arange(context_dev, dtype=jnp.int32))[
        None, :
    ] < cached_length[:, None]
    old_scores = jnp.where(usable[:, None, None, :], old_scores, masked_score)
    row_peak = jnp.maximum(jnp.max(old_scores, axis=-1), jnp.max(new_scores, axis=-1))
    old_weights = jnp.exp(old_scores - row_peak[..., None])
    new_weights = jnp.exp(new_scores - row_peak[..., None])
    row_total = jnp.sum(old_weights, axis=-1) + jnp.sum(new_weights, axis=-1)
    weighted = jnp.einsum(
        "bhgl,blhd->bhgd",
        old_weights.astype(jnp.bfloat16),
        prior_values,
        preferred_element_type=jnp.float32,
    )
    weighted = weighted + jnp.einsum(
        "bhgl,blhd->bhgd",
        new_weights.astype(jnp.bfloat16),
        incoming_values,
        preferred_element_type=jnp.float32,
    )
    row_peak = row_peak.reshape(decode_rows, head_total)
    row_total = row_total.reshape(decode_rows, head_total)
    weighted = weighted.reshape(decode_rows, head_total, HEAD_WIDTH)
    collected = in_one_piece_2((row_peak[None], row_total[None], weighted[None]), "tensor", 2, 0, 3)
    head_peak = jnp.max(collected[0], axis=0)
    factor = jnp.exp(collected[0] - head_peak[None])
    summed_total = jnp.sum(collected[1] * factor, axis=0)
    summed_weighted = jnp.sum(collected[2] * factor[..., None], axis=0)
    own_heads = summed_weighted / summed_total[..., None]
    return own_heads.reshape(decode_rows, local_heads * HEAD_WIDTH).astype(jnp.bfloat16)


def solution(mesh):
    placed = (
        P("group", "tensor"),
        P("tensor", None),
        P("tensor", None),
        P("group", "tensor", None),
        P("group", None),
        P(None, "tensor"),
        P("group", "tensor", None),
        P("group", "tensor", None),
        P("group"),
    )
    return jax.shard_map(
        per_device, mesh=mesh, in_specs=placed, out_specs=P("group", "tensor"), check_vma=False
    )
```

profile of v0, /device:TPU:1, one launch (start us, length us, event | category | flops | bytes accessed | tf_op | source)
XLA Modules:
  0.0 311.5 jit_solution(14728317221646004623)
XLA Ops:
  6.5 3.1 %pad_maximum_fusion = bf16[512,2048]{1,0:T(8,128)(2,1)} fusion(bf16[512,1024]{1,0:T(8,128)(2,1)} %param.11, bf16[512,1024]{1,0:T(8,128)(2,1)} %param.10), kind=kLoop, calls=%fused_computation.12 | loop fusion | flops 4194304 | bytes 4194304 | tf_op jit(solution)/shard_map/concatenate | solution.py:15
  9.7 9.3 %all-to-all-start.1 = ((bf16[16,256,512]{2,1,0:T(8,128)(2,1)}), bf16[16,256,512]{2,1,0:T(8,128)(2,1)}, u32[]{:S(2)}, u32[]{:S(2)}) async-start(bf16[16,256,512]{2,1,0:T(8,128)(2,1)} %bitcast.72), calls=%async_computation.1 | async-start | bytes 8388608 | tf_op jit(solution)/shard_map/all_to_all | solution.py:98
  19.0 4.6 %fusion.58 = f32[4,512]{1,0:T(4,128)S(1)} fusion(bf16[4,8192]{1,0:T(4,128)(2,1)S(1)} %copy-done, bf16[8192,512]{1,0:T(8,128)(2,1)} %param.14), kind=kOutput, calls=%fused_computation.72 | convolution fusion | flops 33554432 | bytes 8462336 | tf_op jit(solution)/shard_map/dot_general | solution.py:130
  23.9 68.5 %all-to-all-done.1 = bf16[16,256,512]{2,1,0:T(8,128)(2,1)} async-done(((bf16[16,256,512]{2,1,0:T(8,128)(2,1)}), bf16[16,256,512]{2,1,0:T(8,128)(2,1)}, u32[]{:S(2)}, u32[]{:S(2)}) %all-to-all-start.1) | async-done | bytes 4194336 | tf_op jit(solution)/shard_map/all_to_all | solution.py:98
  92.4 0.6 broadcast_in_dim.11
  93.0 10.6 %all-to-all-start = ((bf16[16,4,512]{2,1,0:T(4,128)(2,1)}), bf16[16,4,512]{2,1,0:T(4,128)(2,1)S(1)}, u32[]{:S(2)}, u32[]{:S(2)}) async-start(bf16[16,4,512]{2,1,0:T(4,128)(2,1)} %broadcast_in_dim.11), calls=%async_computation | async-start | bytes 131072 | tf_op jit(solution)/shard_map/all_to_all | solution.py:32
  103.7 6.4 %copy.89 = bf16[256,16,512]{0,2,1:T(8,128)(2,1)} copy(bf16[256,16,512]{2,0,1:T(8,128)(2,1)} %bitcast.3) | data formatting | bytes 8388608 | tf_op jit(solution)/shard_map/all_to_all | solution.py:98
  110.1 124.1 %all-gather.2.cloned.1.call-done = bf16[8192,2048]{1,0:T(8,128)(2,1)} async-done(((bf16[512,2048]{1,0:T(8,128)(2,1)}), bf16[8192,2048]{1,0:T(8,128)(2,1)}) %all-gather.2.cloned.1.call-update) | async-done | bytes 33554448 | tf_op jit(solution)/shard_map/all_gather | solution.py:16
  234.2 11.5 %fusion.16 = bf16[256,1024]{0,1:T(8,128)(2,1)S(1)} fusion(bf16[256,8192]{0,1:T(8,128)(2,1)} %bitcast.73, bf16[8192,2048]{1,0:T(8,128)(2,1)} %all-gather.2.cloned.1.call-done), kind=kOutput, calls=%fused_computation.15 | convolution fusion | flops 4295229440 | bytes 21495808 | tf_op jit(solution)/shard_map/dot_general | solution.py:101
  246.2 11.5 %fusion.19 = bf16[256,1024]{0,1:T(8,128)(2,1)S(1)} fusion(bf16[256,8192]{0,1:T(8,128)(2,1)} %bitcast.74, bf16[8192,2048]{1,0:T(8,128)(2,1)} %all-gather.2.cloned.1.call-done), kind=kOutput, calls=%fused_computation.16 | convolution fusion | flops 4295229440 | bytes 21495808 | tf_op jit(solution)/shard_map/dot_general | solution.py:100
  258.8 1.2 all_to_all.43
  260.0 4.0 %all-to-all-start.2 = ((bf16[8,4,16384]{2,1,0:T(4,128)(2,1)}), bf16[8,4,16384]{2,1,0:T(4,128)(2,1)S(1)}, u32[]{:S(2)}, u32[]{:S(2)}) async-start(bf16[8,4,16384]{2,1,0:T(4,128)(2,1)} %all_to_all.43), calls=%async_computation.2 | async-start | bytes 2097152 | tf_op jit(solution)/shard_map/all_to_all | solution.py:26
  264.2 0.5 multiply_cosine_fusion
  264.8 3.5 %fusion.56 = (f32[4,8,8]{2,1,0:T(8,128)S(1)}, f32[4,8,8,512]{3,2,1,0:T(8,128)S(1)}) fusion(bf16[4,8,8,128]{3,2,1,0:T(8,128)(2,1)S(1)} %reshape_reshape.3, pred[4,512]{1,0:T(4,128)(4,1)S(1)} %broadcast_compare_fusion, bf16[4,512,1024]{2,1,0:T(8,128)(2,1)} %param.15), kind=kOutput, calls=%fused_computation.70 | convolution fusion | flops 33947392 | bytes 4787200 | tf_op jit(solution)/shard_map/bhgd,blhd->bhgl/dot_general | solution.py:149
  268.3 11.1 %all-to-all-done.2 = bf16[8,4,16384]{2,1,0:T(4,128)(2,1)S(1)} async-done(((bf16[8,4,16384]{2,1,0:T(4,128)(2,1)}), bf16[8,4,16384]{2,1,0:T(4,128)(2,1)S(1)}, u32[]{:S(2)}, u32[]{:S(2)}) %all-to-all-start.2) | async-done | bytes 1048608 | tf_op jit(solution)/shard_map/all_to_all | solution.py:26
  279.6 1.1 slice_convert_fusion
  280.7 1.4 reshape.222
  282.4 0.4 subtract_convert_fusion
  282.9 0.5 fusion.57
  284.7 3.0 fusion.31
  288.3 13.8 %all_to_all.54 = f32[1,4,64,130]{3,1,0,2:T(4,128)S(1)} all-to-all(f32[1,4,64,130]{3,1,0,2:T(4,128)S(1)} %pad_maximum_fusion.2), channel_id=1, replica_groups=mesh['group'=8,'tensor'=16] {'tensor'}, dimensions={2} | all-to-all | bytes 266240 | tf_op jit(solution)/shard_map/all_to_all | solution.py:52
  302.1 0.7 copy.99
  303.2 0.6 fusion.34
  303.9 0.7 fusion.53
  (49 shorter events, 5.1 us)
Async XLA Ops:
  6.5 12.5 %copy-start = (bf16[4,8192]{1,0:T(4,128)(2,1)S(1)}, bf16[4,8192]{1,0:T(4,128)(2,1)}, u32[]{:S(2)}) copy-start(bf16[4,8192]{1,0:T(4,128)(2,1)} %param.13) | copy-start | bytes 196612
  6.5 227.7 %all-gather.2.cloned.1.call-start = ((), (), s32[]{:S(2)}) async-start(), calls=%async_computation.4 | async-start | bytes 35651584 | tf_op jit(solution)/shard_map/all_gather | solution.py:16
  9.7 82.7 %all-to-all-start.1 = ((bf16[16,256,512]{2,1,0:T(8,128)(2,1)}), bf16[16,256,512]{2,1,0:T(8,128)(2,1)}, u32[]{:S(2)}, u32[]{:S(2)}) async-start(bf16[16,256,512]{2,1,0:T(8,128)(2,1)} %bitcast.72), calls=%async_computation.1 | async-start | bytes 8388608 | tf_op jit(solution)/shard_map/all_to_all | solution.py:98
  19.0 4.6 %copy-start.3 = (s32[4]{0:T(128)S(1)}, s32[4]{0:T(128)}, u32[]{:S(2)}) copy-start(s32[4]{0:T(128)} %param.17) | copy-start | bytes 52
  93.0 167.0 %all-to-all-start = ((bf16[16,4,512]{2,1,0:T(4,128)(2,1)}), bf16[16,4,512]{2,1,0:T(4,128)(2,1)S(1)}, u32[]{:S(2)}, u32[]{:S(2)}) async-start(bf16[16,4,512]{2,1,0:T(4,128)(2,1)} %broadcast_in_dim.11), calls=%async_computation | async-start | bytes 131072 | tf_op jit(solution)/shard_map/all_to_all | solution.py:32
  246.2 12.0 %copy-start.2 = (s32[1,1,32]{2,1,0:T(1,128)S(1)}, s32[1,1,32]{2,1,0:T(1,128)}, u32[]{:S(2)}) copy-start(s32[1,1,32]{2,1,0:T(1,128)} %param.12) | copy-start | bytes 388
  260.0 19.3 %all-to-all-start.2 = ((bf16[8,4,16384]{2,1,0:T(4,128)(2,1)}), bf16[8,4,16384]{2,1,0:T(4,128)(2,1)S(1)}, u32[]{:S(2)}, u32[]{:S(2)}) async-start(bf16[8,4,16384]{2,1,0:T(4,128)(2,1)} %all_to_all.43), calls=%async_computation.2 | async-start | bytes 2097152 | tf_op jit(solution)/shard_map/all_to_all | solution.py:26
  284.4 20.2 %copy-start.1 = (bf16[4,8192]{1,0:T(4,128)(2,1)S(1)}, bf16[4,8192]{1,0:T(4,128)(2,1)}, u32[]{:S(2)}) copy-start(bf16[4,8192]{1,0:T(4,128)(2,1)} %param.13) | copy-start | bytes 196612
Sparse Core Ops, SparseCore 0:
  9.8 224.3 all-gather.1
where the time goes:
time: 312 us; the launch traced here: 311 us
  waiting for transfers between devices  204 us (65%)
  matrix products  35.4 us (11%)
  starting transfers between devices  23.9 us (8%)
  blocking collectives  13.8 us (4%)
  between operations  13.6 us (4%)
  local copies, waits for them, and re-layouts  12.9 us (4%)
  other arithmetic  8.11 us (3%)
    all_gather x1, waiting for transfers between devices, in_one_piece(): lax.all_gather(both, axis, axis=dim, tiled=True)  124 us
    all_to_all x1, waiting for transfers between devices, per_device(): lax.all_to_all(prefill_states, 'tensor', split_axis=0, concat_axis=1, til...  68.5 us
    all_to_all x1, blocking collectives, in_one_piece_2(): lax.all_to_all(both, axis, split_axis=split_dim, concat_axis=concat_dim,...  13.8 us
    dot_general x1, matrix products, per_device(): jnp.dot(token_block, pieces[0], preferred_element_type=jnp.float32)  11.5 us
    dot_general x1, matrix products, per_device(): jnp.dot(token_block, pieces[1], preferred_element_type=jnp.float32)  11.5 us
    all_to_all x1, waiting for transfers between devices, side_by_side(): lax.all_to_all(both, axis, split_axis=split_dim, concat_axis=concat_dim,...  11.1 us
    all_to_all x1, starting transfers between devices, sent_to_all(): lax.all_to_all(jnp.broadcast_to(array[None], (devices, *array.shape)), ax...  10.6 us
    all_to_all x1, starting transfers between devices, per_device(): lax.all_to_all(prefill_states, 'tensor', split_axis=0, concat_axis=1, til...  9.29 us
  transfers between devices with their start and end apart: 4, of which 3 were waited for; matrix products, arithmetic and copies ran while one was open for 13% of the time, Pallas kernels for 0%

commit v1 on v0

v1 whole, which is shorter than its diff:
```python
import jax
import jax.numpy as jnp
import numpy as np
from jax import lax
from jax.experimental import pallas as pl
from jax.experimental.pallas import tpu as pltpu
from jax.sharding import PartitionSpec as P

HEAD_WIDTH = 128
PAGE = 8
BOTH = ("group", "tensor")

rope_theta = 500000.0
masked_score = -1e30

bf16 = jnp.bfloat16
f32 = jnp.float32

HALF = HEAD_WIDTH // 2
FREQUENCY = rope_theta ** (-2.0 * np.arange(HALF) / HEAD_WIDTH)
FREQUENCY_PAIR = np.concatenate([FREQUENCY, FREQUENCY]).astype(np.float32)
SIGN_PAIR = np.concatenate([-np.ones(HALF), np.ones(HALF)]).astype(np.float32)


def sent_to_all(array, axis):
    devices = lax.axis_size(axis)
    return lax.all_to_all(
        jnp.broadcast_to(array[None], (devices, *array.shape)), axis, 0, 0, tiled=True
    )


def apply_rotary(vectors, positions):
    angles = positions[..., None].astype(f32) * FREQUENCY.astype(np.float32)
    cosine_part = jnp.cos(angles)
    sine_part = jnp.sin(angles)
    first_half = vectors[..., :HALF]
    second_half = vectors[..., HALF:]
    return jnp.concatenate(
        [
            first_half * cosine_part - second_half * sine_part,
            second_half * cosine_part + first_half * sine_part,
        ],
        axis=-1,
    )


def partial_keys(states, weight, cosine, sine):
    tokens, features = states.shape
    blocks = cosine.shape[0]
    rows = tokens // blocks
    width = weight.shape[1]
    step = 2 * HEAD_WIDTH

    def kernel(x_ref, w_ref, c_ref, s_ref, o_ref):
        x = x_ref[...]
        c = c_ref[0][None]
        s = s_ref[0][None]
        for at in range(0, width, step):
            k = jnp.dot(x, w_ref[:, at : at + step], preferred_element_type=f32)
            for h in range(0, step, HEAD_WIDTH):
                part = k[:, h : h + HEAD_WIDTH].reshape(rows // PAGE, PAGE, HEAD_WIDTH)
                turned = part * c + pltpu.roll(part, HALF, 2) * s
                o_ref[:, at + h : at + h + HEAD_WIDTH] = turned.reshape(rows, HEAD_WIDTH).astype(bf16)

    return pl.pallas_call(
        kernel,
        out_shape=jax.ShapeDtypeStruct((tokens, width), bf16),
        grid=(blocks,),
        in_specs=[
            pl.BlockSpec((rows, features), lambda i: (i, 0)),
            pl.BlockSpec((features, width), lambda i: (0, 0)),
            pl.BlockSpec((1, PAGE, HEAD_WIDTH), lambda i: (i, 0, 0)),
            pl.BlockSpec((1, PAGE, HEAD_WIDTH), lambda i: (i, 0, 0)),
        ],
        out_specs=pl.BlockSpec((rows, width), lambda i: (i, 0)),
        name="partial_keys",
    )(states, weight, cosine, sine)


def gather_pages(order, pages_ref, buf, sem, row, slot, count):
    for p in range(count):
        pltpu.make_async_copy(
            pages_ref.at[order[row * count + p]], buf.at[slot, p], sem.at[slot]
        ).start()


def wait_pages(pages_ref, buf, sem, slot, count):
    pltpu.make_async_copy(pages_ref.at[pl.ds(0, count)], buf.at[slot], sem.at[slot]).wait()


def partial_scores(order, keys, queries, tables):
    tokens, width = keys.shape
    rows, heads, _ = queries.shape
    per_row = tokens // rows
    count = per_row // PAGE
    turns = tables.shape[1]
    per_turn = per_row // turns
    kv_heads = width // HEAD_WIDTH
    group = heads // kv_heads
    pages = keys.reshape(tokens // PAGE, PAGE, width)

    def kernel(order, pages_ref, q_ref, t_ref, o_ref, buf, sem):
        row = pl.program_id(0)
        slot = lax.rem(row, 2)

        @pl.when(row == 0)
        def _():
            gather_pages(order, pages_ref, buf, sem, 0, 0, count)

        @pl.when(row + 1 < rows)
        def _():
            gather_pages(order, pages_ref, buf, sem, row + 1, 1 - slot, count)

        q = q_ref[0].astype(f32)
        swapped = pltpu.roll(q, HALF, 1)
        own = (
            lax.broadcasted_iota(jnp.int32, (heads, width), 1) // HEAD_WIDTH
            == lax.broadcasted_iota(jnp.int32, (heads, width), 0) // group
        )
        wait_pages(pages_ref, buf, sem, slot, count)
        for m in range(turns):
            turned = q * t_ref[0, m][None] + swapped * t_ref[1, m][None]
            spread = jnp.where(own, jnp.concatenate([turned] * kv_heads, axis=1), 0.0).astype(bf16)
            n = per_turn // PAGE
            k = buf[slot, m * n : (m + 1) * n].reshape(per_turn, width)
            s = lax.dot_general(spread, k, (((1,), (1,)), ((), ())), preferred_element_type=f32)
            o_ref[0, :, m * per_turn : (m + 1) * per_turn] = s.astype(bf16)

    return pl.pallas_call(
        kernel,
        out_shape=jax.ShapeDtypeStruct((rows, heads, per_row), bf16),
        grid_spec=pltpu.PrefetchScalarGridSpec(
            num_scalar_prefetch=1,
            grid=(rows,),
            in_specs=[
                pl.BlockSpec(memory_space=pl.ANY),
                pl.BlockSpec((1, heads, HEAD_WIDTH), lambda i, _: (i, 0, 0)),
                pl.BlockSpec(tables.shape, lambda i, _: (0, 0, 0)),
            ],
            out_specs=pl.BlockSpec((1, heads, per_row), lambda i, _: (i, 0, 0)),
            scratch_shapes=[
                pltpu.VMEM((2, count, PAGE, width), bf16),
                pltpu.SemaphoreType.DMA((2,)),
            ],
        ),
        name="partial_scores",
    )(order, pages, queries, tables)


def sorted_states(order, states, rows):
    tokens, features = states.shape
    per_row = tokens // rows
    count = per_row // PAGE
    pages = states.reshape(tokens // PAGE, PAGE, features)

    def kernel(order, pages_ref, o_ref, buf, sem):
        row = pl.program_id(0)
        slot = lax.rem(row, 2)

        @pl.when(row == 0)
        def _():
            gather_pages(order, pages_ref, buf, sem, 0, 0, count)

        @pl.when(row + 1 < rows)
        def _():
            gather_pages(order, pages_ref, buf, sem, row + 1, 1 - slot, count)

        wait_pages(pages_ref, buf, sem, slot, count)
        o_ref[0] = buf[slot].reshape(per_row, features)

    return pl.pallas_call(
        kernel,
        out_shape=jax.ShapeDtypeStruct((rows, per_row, features), bf16),
        grid_spec=pltpu.PrefetchScalarGridSpec(
            num_scalar_prefetch=1,
            grid=(rows,),
            in_specs=[pl.BlockSpec(memory_space=pl.ANY)],
            out_specs=pl.BlockSpec((1, per_row, features), lambda i, _: (i, 0, 0)),
            scratch_shapes=[
                pltpu.VMEM((2, count, PAGE, features), bf16),
                pltpu.SemaphoreType.DMA((2,)),
            ],
        ),
        name="sorted_states",
    )(order, pages)


def fresh_weights(pieces):
    devices, heads, length = pieces.shape

    def kernel(p_ref, w_ref, s_ref):
        scores = p_ref[0].astype(f32)
        for d in range(1, devices):
            scores = scores + p_ref[d].astype(f32)
        peak = jnp.max(scores, axis=-1, keepdims=True)
        weights = jnp.exp(scores - peak).astype(bf16)
        total = jnp.sum(weights.astype(f32), axis=-1, keepdims=True)
        for d in range(devices):
            w_ref[d] = weights
        lane = lax.broadcasted_iota(jnp.int32, (heads, HEAD_WIDTH), 1)
        head = lax.broadcasted_iota(jnp.int32, (heads, HEAD_WIDTH), 0)
        spread = jnp.where(lane == head, peak, 0.0) + jnp.where(lane == head + heads, total, 0.0)
        s_ref[...] = jnp.broadcast_to(jnp.sum(spread, axis=0, keepdims=True), s_ref.shape)

    return pl.pallas_call(
        kernel,
        out_shape=(
            jax.ShapeDtypeStruct(pieces.shape, bf16),
            jax.ShapeDtypeStruct((8, HEAD_WIDTH), f32),
        ),
        name="fresh_weights",
    )(pieces)


def partial_outputs(weights, states, value_weight, stats, receivers):
    rows, heads, per_row = weights.shape
    features, width = value_weight.shape
    kv_heads = width // HEAD_WIDTH
    group = heads // kv_heads
    local = heads // receivers
    per_kv = group // local

    def kernel(w_ref, x_ref, v_ref, s_ref, o_ref, held, out, lanes):
        row = pl.program_id(0)
        y = jnp.dot(w_ref[0], x_ref[0], preferred_element_type=f32)
        at = pl.multiple_of(row * group, group)
        for j in range(kv_heads):
            held[j, pl.ds(at, group), :] = y[j * group : (j + 1) * group]

        @pl.when(row == rows - 1)
        def _():
            o_ref[:, local * HEAD_WIDTH :] = jnp.broadcast_to(
                s_ref[0:1], (rows * receivers, HEAD_WIDTH)
            )
            for j in range(kv_heads):
                out[j] = jnp.dot(
                    held[j].astype(bf16),
                    v_ref[:, j * HEAD_WIDTH : (j + 1) * HEAD_WIDTH],
                    preferred_element_type=f32,
                )
                for e in range(per_kv):
                    for c in range(local):
                        lanes[c, pl.ds(j * per_kv + e, rows, stride=receivers), :] = out[
                            j, pl.ds(e * local + c, rows, stride=group), :
                        ]
            for c in range(local):
                o_ref[:, c * HEAD_WIDTH : (c + 1) * HEAD_WIDTH] = lanes[c]

    return pl.pallas_call(
        kernel,
        out_shape=jax.ShapeDtypeStruct((rows * receivers, (local + 1) * HEAD_WIDTH), f32),
        grid=(rows,),
        in_specs=[
            pl.BlockSpec((1, heads, per_row), lambda i: (i, 0, 0)),
            pl.BlockSpec((1, per_row, features), lambda i: (i, 0, 0)),
            pl.BlockSpec((features, width), lambda i: (0, 0)),
            pl.BlockSpec((8, HEAD_WIDTH), lambda i: (0, 0)),
        ],
        out_specs=pl.BlockSpec((rows * receivers, (local + 1) * HEAD_WIDTH), lambda i: (0, 0)),
        scratch_shapes=[
            pltpu.VMEM((kv_heads, rows * group, features), f32),
            pltpu.VMEM((kv_heads, rows * group, HEAD_WIDTH), f32),
            pltpu.VMEM((local, rows * receivers, HEAD_WIDTH), f32),
        ],
        name="partial_outputs",
    )(weights, states, value_weight, stats)


def per_device(
    prefill_states,
    key_weight,
    value_weight,
    page_slot,
    decode_states,
    query_weight,
    cache_keys,
    cache_values,
    cached_length,
):
    tensor_size = lax.axis_size("tensor")
    group_size = lax.axis_size("group")
    tensor_rank = lax.axis_index("tensor")
    group_rank = lax.axis_index("group")
    decode_rows = decode_states.shape[0]
    tokens = prefill_states.shape[0]
    kv_width = key_weight.shape[1]
    kv_heads = kv_width // HEAD_WIDTH
    page_count = page_slot.shape[-1]
    per_owner = page_count // group_size
    block = page_count * PAGE
    fresh_per_row = block // decode_rows
    fresh_length = tensor_size * fresh_per_row
    senders_per_row = group_size // decode_rows
    from_sender = fresh_per_row // senders_per_row
    inv_scale = 1.0 / HEAD_WIDTH**0.5

    local_queries = jnp.dot(decode_states, query_weight, preferred_element_type=f32)
    local_width = local_queries.shape[1]
    local_heads = local_width // HEAD_WIDTH
    sent = jnp.repeat(local_queries.astype(bf16), senders_per_row, axis=0)
    slots = jnp.pad(page_slot.reshape(1, page_count).astype(bf16), ((0, 0), (0, 128 - page_count)))
    sent = jnp.concatenate([sent, jnp.broadcast_to(slots, (group_size, 128))], axis=1)
    sent = jnp.broadcast_to(sent[:, None], (group_size, tensor_size, local_width + 128))
    sent = sent.reshape(group_size * tensor_size, local_width + 128)
    received = lax.all_to_all(sent, BOTH, 0, 0, tiled=True)

    first = (group_rank % senders_per_row) * from_sender - fresh_length
    place = (
        jnp.arange(tensor_size, dtype=jnp.int32)[:, None] * fresh_per_row
        + jnp.arange(PAGE, dtype=jnp.int32)[None, :]
        + first
    )
    angles = place[..., None].astype(f32) * FREQUENCY_PAIR
    keys = partial_keys(prefill_states, key_weight, jnp.cos(angles), jnp.sin(angles) * SIGN_PAIR)

    head_total = tensor_size * local_heads
    queries = received[:, :local_width].reshape(group_size, head_total, HEAD_WIDTH)
    slot_of = lax.dynamic_slice(
        received, (group_rank * tensor_size, local_width), (tensor_size, page_count)
    ).astype(jnp.int32)
    index = jnp.arange(page_count, dtype=jnp.int32)
    page_of = jnp.sum(
        jnp.where(slot_of[None] == index[:, None, None], index[None, None, :], 0), axis=-1
    )
    order = (page_of + jnp.arange(tensor_size, dtype=jnp.int32)[None] * page_count).reshape(-1)

    turn = np.arange(per_owner)[:, None] * PAGE * np.concatenate([FREQUENCY, FREQUENCY])[None]
    tables = np.stack([np.cos(turn), -np.sin(turn) * SIGN_PAIR]).astype(np.float32) * np.float32(
        inv_scale
    )
    scores = partial_scores(order, keys, queries, jnp.asarray(tables))
    half = head_total * group_size // tensor_size
    fresh_row = scores.shape[-1]
    pieces = lax.all_to_all(
        scores.reshape(tensor_size, half, fresh_row), "tensor", 0, 0, tiled=True
    )

    states = sorted_states(order, prefill_states, group_size)

    query_position = cached_length + fresh_length
    own_queries = (
        apply_rotary(
            local_queries.reshape(decode_rows, local_heads, HEAD_WIDTH), query_position[:, None]
        )
        .reshape(decode_rows, local_width)
        .astype(bf16)
    )
    own_queries = jnp.moveaxis(sent_to_all(own_queries, "tensor"), 0, 1)
    grouped = own_queries.reshape(decode_rows, kv_heads, head_total // kv_heads, HEAD_WIDTH)
    context_dev = cache_keys.shape[1]
    prior_keys = cache_keys.reshape(decode_rows, context_dev, kv_heads, HEAD_WIDTH)
    prior_values = cache_values.reshape(decode_rows, context_dev, kv_heads, HEAD_WIDTH)
    old_scores = (
        jnp.einsum("bhgd,blhd->bhgl", grouped, prior_keys, preferred_element_type=f32) * inv_scale
    )
    usable = (tensor_rank * context_dev + jnp.arange(context_dev, dtype=jnp.int32))[
        None, :
    ] < cached_length[:, None]
    old_scores = jnp.where(usable[:, None, None, :], old_scores, masked_score)
    row_peak = jnp.max(old_scores, axis=-1)
    old_weights = jnp.exp(old_scores - row_peak[..., None])
    row_total = jnp.sum(old_weights, axis=-1)
    weighted = jnp.einsum(
        "bhgl,blhd->bhgd", old_weights.astype(bf16), prior_values, preferred_element_type=f32
    )
    shape = (decode_rows, tensor_size, local_heads)
    weighted = weighted.reshape(*shape, HEAD_WIDTH)
    old = jnp.concatenate(
        [
            jnp.moveaxis(weighted, 1, 0).reshape(tensor_size, decode_rows * local_heads, HEAD_WIDTH),
            jnp.pad(
                jnp.stack(
                    [
                        jnp.moveaxis(a.reshape(shape), 1, 0).reshape(tensor_size, -1)
                        for a in (row_peak, row_total)
                    ],
                    axis=1,
                ),
                ((0, 0), (0, 0), (0, HEAD_WIDTH - decode_rows * local_heads)),
            ),
        ],
        axis=1,
    )
    old = lax.all_to_all(old, "tensor", 0, 0, tiled=True)

    weights, stats = fresh_weights(pieces)
    weights = lax.all_to_all(weights, "tensor", 0, 0, tiled=True)
    weights = weights.reshape(group_size, head_total, fresh_row)
    outputs = partial_outputs(weights, states, value_weight, stats, tensor_size)
    outputs = lax.all_to_all(outputs, BOTH, 0, 0, tiled=True)

    own = decode_rows * local_heads
    old_stats = old[:, own:, :own].reshape(tensor_size, 2, decode_rows, local_heads)
    old_peak = jnp.max(old_stats[:, 0], axis=0)
    factor = jnp.exp(old_stats[:, 0] - old_peak[None])
    old_total = jnp.sum(old_stats[:, 1] * factor, axis=0)
    old_sum = jnp.sum(
        old[:, :own].reshape(tensor_size, decode_rows, local_heads, HEAD_WIDTH)
        * factor[..., None],
        axis=0,
    )
    outputs = outputs.reshape(group_size, tensor_size, local_width + HEAD_WIDTH)
    fresh_sum = jnp.sum(outputs[:, :, :local_width], axis=1).reshape(
        decode_rows, senders_per_row, local_heads, HEAD_WIDTH
    )
    per_source = half // local_heads
    source = group_rank * (tensor_size // group_size) + tensor_rank // per_source
    head_at = local_width + (tensor_rank % per_source) * local_heads
    fresh_peak, fresh_total = (
        lax.dynamic_slice(outputs, (0, source, at), (group_size, 1, local_heads)).reshape(
            decode_rows, senders_per_row, local_heads
        )
        for at in (head_at, head_at + half)
    )
    peak = jnp.maximum(old_peak, jnp.max(fresh_peak, axis=1))
    fresh_factor = jnp.exp(fresh_peak - peak[:, None])
    old_factor = jnp.exp(old_peak - peak)
    total = old_total * old_factor + jnp.sum(fresh_total * fresh_factor, axis=1)
    summed = old_sum * old_factor[..., None] + jnp.sum(fresh_sum * fresh_factor[..., None], axis=1)
    return (summed / total[..., None]).reshape(decode_rows, local_width).astype(bf16)


def solution(mesh):
    placed = (
        P("group", "tensor"),
        P("tensor", None),
        P("tensor", None),
        P("group", "tensor", None),
        P("group", None),
        P(None, "tensor"),
        P("group", "tensor", None),
        P("group", "tensor", None),
        P("group"),
    )
    return jax.shard_map(
        per_device, mesh=mesh, in_specs=placed, out_specs=P("group", "tensor"), check_vma=False
    )
```

time: 312 us -> 140 us (0.45)
  waiting for transfers between devices: 204 us -> 35.3 us
  Pallas kernels: 0 us -> 41.6 us
  matrix products: 35.4 us -> 11 us
  blocking collectives: 13.8 us -> 0 us
  between operations: 13.6 us -> 0.3 us
  starting transfers between devices: 23.9 us -> 35.9 us
  other arithmetic: 8.11 us -> 4.25 us
  local copies, waits for them, and re-layouts: 12.9 us -> 9.21 us
    all_gather x1 -> x0, waiting for transfers between devices: 124 us -> none  [in_one_piece(): lax.all_gather(both, axis, axis=dim, tiled=True)]
    all_to_all x2 -> x5, waiting for transfers between devices: 79.5 us -> 35.3 us  [the longest x1 11.7 us: per_device(): outputs = lax.all_to_all(outputs, BOTH, 0, 0, tiled=True)]
    pallas_call x0 -> x5, Pallas kernels: none -> 41.6 us  [the longest x1 15.6 us: partial_keys(): pl.pallas_call(kernel, out_shape=jax.ShapeDtypeStruct((tokens, width), bf...]
    dot_general x8 -> x2, matrix products: 31.9 us -> 7.49 us  [the longest x1 4.56 us: per_device(): jnp.dot(decode_states, query_weight, preferred_element_type=f32)]
    all_to_all x1 -> x0, blocking collectives: 13.8 us -> none  [in_one_piece_2(): lax.all_to_all(both, axis, split_axis=split_dim, concat_axis=concat_dim,...]
    all_to_all x2 -> x5, starting transfers between devices: 13.3 us -> 26.6 us  [the longest x1 9.44 us: per_device(): received = lax.all_to_all(sent, BOTH, 0, 0, tiled=True)]
    all_to_all x4 -> x2, local copies, waits for them, and re-layouts: 8.59 us -> 2.53 us  [the longest x1 2.02 us: per_device(): outputs = lax.all_to_all(outputs, BOTH, 0, 0, tiled=True)]
    concatenate x3 -> x2, other arithmetic: 3.54 us -> 0.02 us  [the longest x1 0.01 us: per_device(): jnp.concatenate([jnp.moveaxis(weighted, 1, 0).reshape(tensor_size, decode...]
  transfers between devices with their start and end apart: 4 -> 6, of which waited for: 3 -> 5; matrix products, arithmetic and copies ran while one was open for 13% -> 9% of each run, Pallas kernels for 0% -> 18%
where the time goes in v1:
time: 140 us; the launch traced here: 138 us
  Pallas kernels  41.6 us (30%)
  starting transfers between devices  35.9 us (26%)
  waiting for transfers between devices  35.3 us (25%)
  matrix products  11 us (8%)
  local copies, waits for them, and re-layouts  9.21 us (7%)
  other arithmetic  4.25 us (3%)
    pallas_call x1, Pallas kernels, partial_keys(): pl.pallas_call(kernel, out_shape=jax.ShapeDtypeStruct((tokens, width), bf...  15.6 us
    all_to_all x1, waiting for transfers between devices, per_device(): outputs = lax.all_to_all(outputs, BOTH, 0, 0, tiled=True)  11.7 us
    pallas_call x1, Pallas kernels, partial_scores(): pl.pallas_call(kernel, out_shape=jax.ShapeDtypeStruct((rows, heads, per_r...  9.55 us
    all_to_all x1, starting transfers between devices, per_device(): received = lax.all_to_all(sent, BOTH, 0, 0, tiled=True)  9.44 us
    all_to_all x1, starting transfers between devices, sent_to_all(): lax.all_to_all(jnp.broadcast_to(array[None], (devices, *array.shape)), ax...  9.28 us
    all_to_all x1, waiting for transfers between devices, per_device(): lax.all_to_all(scores.reshape(tensor_size, half, fresh_row), 'tensor', 0,...  7.54 us
    pallas_call x1, Pallas kernels, sorted_states(): pl.pallas_call(kernel, out_shape=jax.ShapeDtypeStruct((rows, per_row, fea...  7.52 us
    pallas_call x1, Pallas kernels, partial_outputs(): pl.pallas_call(kernel, out_shape=jax.ShapeDtypeStruct((rows * receivers,...  6.97 us
  transfers between devices with their start and end apart: 6, of which 5 were waited for; matrix products, arithmetic and copies ran while one was open for 9% of the time, Pallas kernels for 18%

profile of v1, /device:TPU:1, one launch (start us, length us, event | category | flops | bytes accessed | tf_op | source)
XLA Modules:
  0.0 137.5 jit_solution(14130380630976330411)
XLA Ops:
  0.0 0.8 copy-done
  0.8 4.6 %fusion.23 = (bf16[4,512]{1,0:T(4,128)(2,1)S(1)}, f32[4,512]{1,0:T(4,128)S(1)}) fusion(bf16[4,8192]{1,0:T(4,128)(2,1)S(1)} %copy-done, bf16[8192,512]{1,0:T(8,128)(2,1)} %param.18), kind=kOutput, calls=%fused_computation.62 | convolution fusion | flops 33556480 | bytes 8466432 | tf_op jit(solution)/shard_map/dot_general | solution.py:297
  6.4 9.3 %all-to-all-start = ((bf16[16,4,512]{2,1,0:T(4,128)(2,1)}), bf16[16,4,512]{2,1,0:T(4,128)(2,1)S(1)}, u32[]{:S(2)}, u32[]{:S(2)}) async-start(bf16[16,4,512]{2,1,0:T(4,128)(2,1)} %broadcast_in_dim.31), calls=%async_computation | async-start | bytes 131072 | tf_op jit(solution)/shard_map/all_to_all | solution.py:27
  17.0 0.9 reshape.279
  18.0 1.0 fusion.17
  19.0 15.6 %partial_keys.1 = bf16[4096,1024]{1,0:T(8,128)(2,1)} custom-call(bf16[4096,512]{1,0:T(8,128)(2,1)} %x_ref.1, bf16[512,1024]{1,0:T(8,128)(2,1)} %w_ref.1, f32[16,8,128]{2,1,0:T(8,128)} %get-tuple-element.20.c_ref, f32[16,8,128]{2,1,0:T(8,128)} %get-tuple-element.19.s_ref), custom_call_target="tpu_custom_call" | custom-call | tf_op jit(solution)/shard_map/partial_keys/pallas_call | solution.py:65
  34.6 9.4 %all-to-all-start.2 = ((bf16[128,2,320]{2,1,0:T(2,128)(2,1)}), bf16[128,2,320]{2,1,0:T(2,128)(2,1)S(1)}, u32[]{:S(2)}, u32[]{:S(2)}) async-start(bf16[128,2,320]{2,1,0:T(2,128)(2,1)} %reshape.279), calls=%async_computation.2 | async-start | bytes 393216 | tf_op jit(solution)/shard_map/all_to_all | solution.py:305
  44.1 3.5 %fusion.24 = (f32[4,8,8]{2,1,0:T(8,128)S(1)}, f32[4,8,8,512]{3,2,1,0:T(8,128)S(1)}) fusion(bf16[4,8,8,128]{3,2,1,0:T(8,128)(2,1)S(1)} %reshape.259, pred[4,512]{1,0:T(4,128)(4,1)S(1)} %broadcast_compare_fusion, bf16[4,512,1024]{2,1,0:T(8,128)(2,1)} %param.19), kind=kOutput, calls=%fused_computation.63 | convolution fusion | flops 33947392 | bytes 4787200 | tf_op jit(solution)/shard_map/bhgd,blhd->bhgl/dot_general | solution.py:354
  48.3 6.4 %all-to-all-done.2 = bf16[128,2,320]{2,1,0:T(2,128)(2,1)S(1)} async-done(((bf16[128,2,320]{2,1,0:T(2,128)(2,1)}), bf16[128,2,320]{2,1,0:T(2,128)(2,1)S(1)}, u32[]{:S(2)}, u32[]{:S(2)}) %all-to-all-start.2) | async-done | bytes 163872 | tf_op jit(solution)/shard_map/all_to_all | solution.py:305
  57.1 9.6 %partial_scores.1 = bf16[8,64,512]{2,1,0:T(8,128)(2,1)} custom-call(s32[512]{0:T(512)} %add.114.order, bf16[512,8,1024]{2,1,0:T(8,128)(2,1)} %bitcast.89, bf16[8,64,128]{2,1,0:T(8,128)(2,1)} %reshape.269.q_ref, f32[2,4,128]{2,1,0:T(4,128)} %constant.92.clone.t_ref), custom_call_target="tpu_custom_call" | custom-call | tf_op jit(solution)/shard_map/partial_scores/pallas_call | solution.py:129
  66.7 3.8 %all-to-all-start.3 = ((bf16[16,32,512]{2,1,0:T(8,128)(2,1)}), bf16[16,32,512]{2,1,0:T(8,128)(2,1)S(1)}, u32[]{:S(2)}, u32[]{:S(2)}) async-start(bf16[16,32,512]{2,1,0:T(8,128)(2,1)} %bitcast.91), calls=%async_computation.3 | async-start | bytes 1048576 | tf_op jit(solution)/shard_map/all_to_all | solution.py:334
  70.5 2.9 %fusion = f32[4,8,8,128]{3,2,1,0:T(8,128)S(1)} fusion(f32[4,8,8,512]{3,2,1,0:T(8,128)S(1)} %get-tuple-element.26, f32[4,8,8]{2,1,0:T(8,128)S(1)} %get-tuple-element.25, bf16[4,512,1024]{2,1,0:T(8,128)(2,1)} %param.20), kind=kOutput, calls=%fused_computation | convolution fusion | flops 33816576 | bytes 4850688 | tf_op jit(solution)/shard_map/bhgl,blhd->bhgd/dot_general | solution.py:363
  74.2 7.5 %all-to-all-done.3.p_ref = bf16[16,32,512]{2,1,0:T(8,128)(2,1)S(1)} async-done(((bf16[16,32,512]{2,1,0:T(8,128)(2,1)}), bf16[16,32,512]{2,1,0:T(8,128)(2,1)S(1)}, u32[]{:S(2)}, u32[]{:S(2)}) %all-to-all-start.3) | async-done | bytes 524320 | tf_op jit(solution)/shard_map/all_to_all | solution.py:334
  81.7 4.6 %all-to-all-start.1 = ((f32[16,18,128]{2,1,0:T(8,128)}), f32[16,18,128]{2,1,0:T(8,128)S(1)}, u32[]{:S(2)}, u32[]{:S(2)}) async-start(f32[16,18,128]{2,1,0:T(8,128)} %copy.62), calls=%async_computation.1 | async-start | bytes 393216 | tf_op jit(solution)/shard_map/all_to_all | solution.py:384
  86.3 2.0 %fresh_weights.1 = (bf16[16,32,512]{2,1,0:T(8,128)(2,1)}, f32[8,128]{1,0:T(8,128)}) custom-call(bf16[16,32,512]{2,1,0:T(8,128)(2,1)} %copy-done.1), custom_call_target="tpu_custom_call" | custom-call | tf_op jit(solution)/shard_map/fresh_weights/pallas_call | solution.py:205
  88.3 6.2 %all-to-all-done.1 = f32[16,18,128]{2,1,0:T(8,128)S(1)} async-done(((f32[16,18,128]{2,1,0:T(8,128)}), f32[16,18,128]{2,1,0:T(8,128)S(1)}, u32[]{:S(2)}, u32[]{:S(2)}) %all-to-all-start.1) | async-done | bytes 147488 | tf_op jit(solution)/shard_map/all_to_all | solution.py:384
  94.5 4.2 %all-to-all-start.4 = ((bf16[16,32,512]{2,1,0:T(8,128)(2,1)}), bf16[16,32,512]{2,1,0:T(8,128)(2,1)S(1)}, u32[]{:S(2)}, u32[]{:S(2)}) async-start(bf16[16,32,512]{2,1,0:T(8,128)(2,1)} %get-tuple-element.7), calls=%async_computation.4 | async-start | bytes 1048576 | tf_op jit(solution)/shard_map/all_to_all | solution.py:387
  98.7 7.5 %sorted_states.1.x_ref = bf16[8,512,512]{2,1,0:T(8,128)(2,1)} custom-call(s32[512]{0:T(512)} %add.114.order, bf16[512,8,512]{2,1,0:T(8,128)(2,1)} %bitcast.90), custom_call_target="tpu_custom_call" | custom-call | tf_op jit(solution)/shard_map/sorted_states/pallas_call | solution.py:171
  106.5 3.5 %all-to-all-done.4 = bf16[16,32,512]{2,1,0:T(8,128)(2,1)S(1)} async-done(((bf16[16,32,512]{2,1,0:T(8,128)(2,1)}), bf16[16,32,512]{2,1,0:T(8,128)(2,1)S(1)}, u32[]{:S(2)}, u32[]{:S(2)}) %all-to-all-start.4) | async-done | bytes 524320 | tf_op jit(solution)/shard_map/all_to_all | solution.py:387
  109.9 0.8 copy-done.2
  110.7 7.0 %partial_outputs.1 = f32[128,640]{1,0:T(8,128)} custom-call(bf16[8,64,512]{2,1,0:T(8,128)(2,1)} %bitcast.92, bf16[8,512,512]{2,1,0:T(8,128)(2,1)} %sorted_states.1.x_ref, bf16[512,1024]{1,0:T(8,128)(2,1)} %v_ref.1, f32[8,128]{1,0:T(8,128)} %get-tuple-element.8.s_ref), custom_call_target="tpu_custom_call" | custom-call | tf_op jit(solution)/shard_map/partial_outputs/pallas_call | solution.py:249
  117.7 2.0 %copy.66 = f32[128,1,640]{2,1,0:T(1,128)} copy(f32[128,1,640]{2,0,1:T(8,128)} %bitcast.93) | data formatting | bytes 655360 | tf_op jit(solution)/shard_map/all_to_all | solution.py:390
  119.7 4.7 %all-to-all-start.5 = ((f32[128,1,640]{2,1,0:T(1,128)}), f32[128,1,640]{2,1,0:T(1,128)S(1)}, u32[]{:S(2)}, u32[]{:S(2)}) async-start(f32[128,1,640]{2,1,0:T(1,128)} %copy.66), calls=%async_computation.5 | async-start | bytes 655360 | tf_op jit(solution)/shard_map/all_to_all | solution.py:390
  124.8 11.7 %all-to-all-done.5 = f32[128,1,640]{2,1,0:T(1,128)S(1)} async-done(((f32[128,1,640]{2,1,0:T(1,128)}), f32[128,1,640]{2,1,0:T(1,128)S(1)}, u32[]{:S(2)}, u32[]{:S(2)}) %all-to-all-start.5) | async-done | bytes 327712 | tf_op jit(solution)/shard_map/all_to_all | solution.py:390
  (77 shorter events, 8.0 us)
Async XLA Ops:
  0.0 0.8 copy-start
  0.0 5.4 %copy-start.6 = (f32[64]{0:T(128)S(1)}, f32[64]{0:T(128)}, u32[]{:S(2)}) copy-start(f32[64]{0:T(128)} %constant.93.clone) | copy-start | bytes 772
  0.0 18.0 %copy-start.3 = (f32[128]{0:T(128)S(1)}, f32[128]{0:T(128)}, u32[]{:S(2)}) copy-start(f32[128]{0:T(128)} %constant.90.clone) | copy-start | bytes 1540
  0.0 18.0 %copy-start.4 = (f32[128]{0:T(128)S(1)}, f32[128]{0:T(128)}, u32[]{:S(2)}) copy-start(f32[128]{0:T(128)} %constant.91.clone) | copy-start | bytes 1540
  0.0 5.4 %copy-start.5 = (s32[4]{0:T(128)S(1)}, s32[4]{0:T(128)}, u32[]{:S(2)}) copy-start(s32[4]{0:T(128)} %param.21) | copy-start | bytes 52
  0.0 15.7 %copy-start.7 = (s32[1,1,32]{2,1,0:T(1,128)S(1)}, s32[1,1,32]{2,1,0:T(1,128)}, u32[]{:S(2)}) copy-start(s32[1,1,32]{2,1,0:T(1,128)} %param.16) | copy-start | bytes 388
  6.4 28.2 %all-to-all-start = ((bf16[16,4,512]{2,1,0:T(4,128)(2,1)}), bf16[16,4,512]{2,1,0:T(4,128)(2,1)S(1)}, u32[]{:S(2)}, u32[]{:S(2)}) async-start(bf16[16,4,512]{2,1,0:T(4,128)(2,1)} %broadcast_in_dim.31), calls=%async_computation | async-start | bytes 131072 | tf_op jit(solution)/shard_map/all_to_all | solution.py:27
  34.6 20.2 %all-to-all-start.2 = ((bf16[128,2,320]{2,1,0:T(2,128)(2,1)}), bf16[128,2,320]{2,1,0:T(2,128)(2,1)S(1)}, u32[]{:S(2)}, u32[]{:S(2)}) async-start(bf16[128,2,320]{2,1,0:T(2,128)(2,1)} %reshape.279), calls=%async_computation.2 | async-start | bytes 393216 | tf_op jit(solution)/shard_map/all_to_all | solution.py:305
  66.7 15.0 %all-to-all-start.3 = ((bf16[16,32,512]{2,1,0:T(8,128)(2,1)}), bf16[16,32,512]{2,1,0:T(8,128)(2,1)S(1)}, u32[]{:S(2)}, u32[]{:S(2)}) async-start(bf16[16,32,512]{2,1,0:T(8,128)(2,1)} %bitcast.91), calls=%async_computation.3 | async-start | bytes 1048576 | tf_op jit(solution)/shard_map/all_to_all | solution.py:334
  81.7 4.6 %copy-start.1 = (bf16[16,32,512]{2,1,0:T(8,128)(2,1)}, bf16[16,32,512]{2,1,0:T(8,128)(2,1)S(1)}, u32[]{:S(2)}) copy-start(bf16[16,32,512]{2,1,0:T(8,128)(2,1)S(1)} %all-to-all-done.3.p_ref) | copy-start | bytes 1572868
  81.7 12.8 %all-to-all-start.1 = ((f32[16,18,128]{2,1,0:T(8,128)}), f32[16,18,128]{2,1,0:T(8,128)S(1)}, u32[]{:S(2)}, u32[]{:S(2)}) async-start(f32[16,18,128]{2,1,0:T(8,128)} %copy.62), calls=%async_computation.1 | async-start | bytes 393216 | tf_op jit(solution)/shard_map/all_to_all | solution.py:384
  94.5 15.4 %all-to-all-start.4 = ((bf16[16,32,512]{2,1,0:T(8,128)(2,1)}), bf16[16,32,512]{2,1,0:T(8,128)(2,1)S(1)}, u32[]{:S(2)}, u32[]{:S(2)}) async-start(bf16[16,32,512]{2,1,0:T(8,128)(2,1)} %get-tuple-element.7), calls=%async_computation.4 | async-start | bytes 1048576 | tf_op jit(solution)/shard_map/all_to_all | solution.py:387
  109.9 0.8 copy-start.2
  119.7 16.8 %all-to-all-start.5 = ((f32[128,1,640]{2,1,0:T(1,128)}), f32[128,1,640]{2,1,0:T(1,128)S(1)}, u32[]{:S(2)}, u32[]{:S(2)}) async-start(f32[128,1,640]{2,1,0:T(1,128)} %copy.66), calls=%async_computation.5 | async-start | bytes 655360 | tf_op jit(solution)/shard_map/all_to_all | solution.py:390

commit v2 on v1

v2 whole, which is shorter than its diff:
```python
import jax
import jax.numpy as jnp
import numpy as np
from jax import lax
from jax.experimental import pallas as pl
from jax.experimental.pallas import tpu as pltpu
from jax.sharding import PartitionSpec as P


HEAD_WIDTH = 128
PAGE = 8
BOTH = ("group", "tensor")

rope_theta = 500000.0
masked_score = -1e30

bf16 = jnp.bfloat16
f32 = jnp.float32

HALF = HEAD_WIDTH // 2
FREQUENCY = rope_theta ** (-2.0 * np.arange(HALF) / HEAD_WIDTH)
FREQUENCY_PAIR = np.concatenate([FREQUENCY, FREQUENCY]).astype(np.float32)
SIGN_PAIR = np.concatenate([-np.ones(HALF), np.ones(HALF)]).astype(np.float32)


def apply_rotary(vectors, positions):
    angles = positions[..., None].astype(f32) * FREQUENCY.astype(np.float32)
    cosine_part = jnp.cos(angles)
    sine_part = jnp.sin(angles)
    first_half = vectors[..., :HALF]
    second_half = vectors[..., HALF:]
    return jnp.concatenate(
        [
            first_half * cosine_part - second_half * sine_part,
            second_half * cosine_part + first_half * sine_part,
        ],
        axis=-1,
    )


SMALL = pltpu.CompilerParams(vmem_limit_bytes=32 * 1024 * 1024)


def in_hbm(x):
    return pltpu.with_memory_space_constraint(x, pltpu.HBM)


def exchanged(x, axis):
    return lax.all_to_all(x, axis, 0, 0, tiled=True)


def swap_halves(x):
    return pltpu.roll(x, HALF, x.ndim - 1)


def packed_queries(decode_states, query_weight, page_slot, groups, receivers):
    rows, features = decode_states.shape
    width = query_weight.shape[1]
    heads = width // HEAD_WIDTH
    pages = page_slot.shape[-1]
    steps = 8
    depth = features // steps
    per_row = groups // rows

    def kernel(d_ref, w_ref, s_ref, q_ref, o_ref):
        at = pl.program_id(0)
        part = jnp.dot(d_ref[...], w_ref[...], preferred_element_type=f32)

        @pl.when(at == 0)
        def _():
            q_ref[...] = part

        @pl.when(at > 0)
        def _():
            q_ref[...] += part

        @pl.when(at == steps - 1)
        def _():
            lane = lax.broadcasted_iota(jnp.int32, (pages, pages), 1)
            head = lax.broadcasted_iota(jnp.int32, (pages, pages), 0)
            slot = jnp.sum(jnp.where(lane == head, s_ref[0], 0).astype(f32), axis=1, keepdims=True)
            lanes = lax.broadcasted_iota(jnp.int32, (pages, HEAD_WIDTH), 1).astype(f32)
            page = lax.broadcasted_iota(jnp.int32, (pages, HEAD_WIDTH), 0).astype(f32)
            inverse = jnp.sum(jnp.where(slot == lanes, page, 0.0), axis=0, keepdims=True)
            index = lax.broadcasted_iota(jnp.int32, (8, HEAD_WIDTH), 0)
            for r in range(rows):
                tile = jnp.where(index == heads, inverse, 0.0)
                for c in range(heads):
                    own = q_ref[r : r + 1, c * HEAD_WIDTH : (c + 1) * HEAD_WIDTH]
                    tile = jnp.where(index == c, own, tile)
                n = per_row * receivers
                o_ref[r * n : (r + 1) * n] = jnp.broadcast_to(
                    tile.astype(bf16)[None], (n, 8, HEAD_WIDTH)
                )

    return pl.pallas_call(
        kernel,
        out_shape=(
            jax.ShapeDtypeStruct((rows, width), f32),
            jax.ShapeDtypeStruct((groups * receivers, 8, HEAD_WIDTH), bf16),
        ),
        grid=(steps,),
        in_specs=[
            pl.BlockSpec((rows, depth), lambda i: (0, i)),
            pl.BlockSpec((depth, width), lambda i: (i, 0)),
            pl.BlockSpec((1, 1, pages), lambda i: (0, 0, 0)),
        ],
        out_specs=(
            pl.BlockSpec((rows, width), lambda i: (0, 0)),
            pl.BlockSpec((groups * receivers, 8, HEAD_WIDTH), lambda i: (0, 0, 0)),
        ),
        compiler_params=SMALL,
        name="packed_queries",
    )(decode_states, in_hbm(query_weight), page_slot)


def partial_keys(states, weight, cosine, sine):
    tokens, features = states.shape
    blocks = cosine.shape[0]
    rows = tokens // blocks
    width = weight.shape[1]
    step = 2 * HEAD_WIDTH

    def kernel(x_ref, w_ref, c_ref, s_ref, o_ref, mixed):
        @pl.when(pl.program_id(0) == 0)
        def _():
            low = lax.broadcasted_iota(jnp.int32, (features, HEAD_WIDTH), 1) < HALF
            for at in range(0, width, step):
                one = w_ref[:, at : at + HEAD_WIDTH].astype(f32)
                two = w_ref[:, at + HEAD_WIDTH : at + step].astype(f32)
                mixed[:, at : at + HEAD_WIDTH] = jnp.where(low, one, swap_halves(two)).astype(bf16)
                mixed[:, at + HEAD_WIDTH : at + step] = jnp.where(
                    low, swap_halves(one), two
                ).astype(bf16)

        x = x_ref[...]
        c = c_ref[0][None]
        s = s_ref[0][None]
        for at in range(0, width, step):
            k = jnp.dot(x, mixed[:, at : at + step], preferred_element_type=f32)
            first = k[:, :HEAD_WIDTH].reshape(rows // PAGE, PAGE, HEAD_WIDTH)
            second = k[:, HEAD_WIDTH:].reshape(rows // PAGE, PAGE, HEAD_WIDTH)
            o_ref[:, at : at + HEAD_WIDTH] = (
                (first * c - second * s).reshape(rows, HEAD_WIDTH).astype(bf16)
            )
            o_ref[:, at + HEAD_WIDTH : at + step] = (
                (second * c + first * s).reshape(rows, HEAD_WIDTH).astype(bf16)
            )

    return pl.pallas_call(
        kernel,
        out_shape=pltpu.VMEM((tokens, width), bf16),
        grid=(blocks,),
        in_specs=[
            pl.BlockSpec((rows, features), lambda i: (i, 0)),
            pl.BlockSpec((features, width), lambda i: (0, 0)),
            pl.BlockSpec((1, PAGE, HEAD_WIDTH), lambda i: (i, 0, 0)),
            pl.BlockSpec((1, PAGE, HEAD_WIDTH), lambda i: (i, 0, 0)),
        ],
        out_specs=pl.BlockSpec((rows, width), lambda i: (i, 0)),
        scratch_shapes=[pltpu.VMEM((features, width), bf16)],
        compiler_params=SMALL,
        name="partial_keys",
    )(states, weight, cosine, sine)


def start_pages(order, pages_ref, buf, sem, row, turns, blocks, only=None):
    per_block = order.shape[1]
    for m in range(turns) if only is None else (only,):
        for t in range(blocks):
            page = order[t, row * turns + m] + t * per_block
            pltpu.make_async_copy(pages_ref.at[page], buf.at[m * blocks + t], sem).start()


def wait_pages(pages_ref, buf, sem):
    pltpu.make_async_copy(pages_ref.at[pl.ds(0, buf.shape[0])], buf, sem).wait()


def partial_scores(order, keys, received, own_queries, tables, rows):
    tokens, width = keys.shape
    blocks, page_count = order.shape
    senders = received.shape[0] // rows
    local = own_queries.shape[1] // HEAD_WIDTH
    own_rows = own_queries.shape[0]
    heads = senders * local
    per_row = tokens // rows
    turns = tables.shape[1]
    per_turn = per_row // turns
    kv_heads = width // HEAD_WIDTH
    group = heads // kv_heads
    half = heads // 2
    pages = keys.reshape(tokens // PAGE, PAGE, width)

    def kernel(order, k_ref, r_ref, own_ref, t_ref, o_ref, line, chosen):
        row = pl.program_id(0)
        for m in range(turns):
            for t in range(blocks):
                page = order[t, row * turns + m] + t * page_count
                chosen[m * blocks + t] = k_ref[page]
        pair = lax.broadcasted_iota(jnp.int32, (heads, width), 1)
        head = lax.broadcasted_iota(jnp.int32, (heads, width), 0) // group
        mask = (pair // (2 * HEAD_WIDTH) == head // 2) & (
            lax.rem(pair, HEAD_WIDTH) // HALF == lax.rem(head, 2)
        )
        low = lax.broadcasted_iota(jnp.int32, (heads, HEAD_WIDTH), 1) < HALF
        for c in range(local):
            line[pl.ds(c, senders, stride=local), :] = r_ref[:, c, :].astype(f32)
        q = line[...]
        other = swap_halves(q)
        first = jnp.where(low, q, other)
        second = jnp.where(low, other, q)
        for m in range(turns):
            one = first * t_ref[0, m][None] + second * t_ref[1, m][None]
            two = second * t_ref[0, m][None] - first * t_ref[1, m][None]
            spread = jnp.where(
                mask, jnp.concatenate([one, two] * (kv_heads // 2), axis=1), 0.0
            ).astype(bf16)
            k = chosen[m * blocks : (m + 1) * blocks].reshape(per_turn, width)
            s = lax.dot_general(
                spread, k, (((1,), (1,)), ((), ())), preferred_element_type=f32
            ).astype(bf16)
            for e in range(2):
                o_ref[e, :half, m * per_turn : (m + 1) * per_turn] = s[e * half : (e + 1) * half]
        for e in range(2):
            o_ref[e, half:, :] = own_ref[...]

    own = jnp.pad(own_queries, ((0, 8 - own_rows), (0, 0)))
    return pl.pallas_call(
        kernel,
        out_shape=jax.ShapeDtypeStruct((rows * 2, half + 8, per_row), bf16),
        grid_spec=pltpu.PrefetchScalarGridSpec(
            num_scalar_prefetch=1,
            grid=(rows,),
            in_specs=[
                pl.BlockSpec(memory_space=pltpu.VMEM),
                pl.BlockSpec((senders, 8, HEAD_WIDTH), lambda i, _: (i, 0, 0)),
                pl.BlockSpec(own.shape, lambda i, _: (0, 0)),
                pl.BlockSpec(tables.shape, lambda i, _: (0, 0, 0)),
            ],
            out_specs=pl.BlockSpec((2, half + 8, per_row), lambda i, _: (i, 0, 0)),
            scratch_shapes=[
                pltpu.VMEM((heads, HEAD_WIDTH), f32),
                pltpu.VMEM((turns * blocks, PAGE, width), bf16),
            ],
        ),
        compiler_params=SMALL,
        name="partial_scores",
    )(order, pages, received, own, tables)


def sorted_states(order, states, rows, turns):
    tokens, features = states.shape
    blocks = order.shape[0]
    per_row = tokens // rows
    count = per_row // PAGE
    pages = in_hbm(states.reshape(tokens // PAGE, PAGE, features))

    def kernel(order, pages_ref, o_ref, buf, sem):
        row = pl.program_id(0)
        slot = lax.rem(row, 2)

        @pl.when(row == 0)
        def _():
            start_pages(order, pages_ref, buf.at[0], sem.at[0], 0, turns, blocks)

        @pl.when(row + 1 < rows)
        def _():
            start_pages(order, pages_ref, buf.at[1 - slot], sem.at[1 - slot], row + 1, turns, blocks)

        wait_pages(pages_ref, buf.at[slot], sem.at[slot])
        o_ref[0] = buf[slot].reshape(per_row, features)

    return pl.pallas_call(
        kernel,
        out_shape=pltpu.HBM((rows, per_row, features), bf16),
        grid_spec=pltpu.PrefetchScalarGridSpec(
            num_scalar_prefetch=1,
            grid=(rows,),
            in_specs=[pl.BlockSpec(memory_space=pl.ANY)],
            out_specs=pl.BlockSpec((1, per_row, features), lambda i, _: (i, 0, 0)),
            scratch_shapes=[
                pltpu.VMEM((2, count, PAGE, features), bf16),
                pltpu.SemaphoreType.DMA((2,)),
            ],
        ),
        compiler_params=SMALL,
        name="sorted_states",
    )(order, pages)


def thirds(x):
    high = x.astype(bf16).astype(f32)
    rest = x - high
    middle = rest.astype(bf16).astype(f32)
    return high, middle, (rest - middle).astype(bf16).astype(f32)


def fresh_weights(pieces, heads):
    devices, _, length = pieces.shape

    def kernel(p_ref, w_ref, s_ref):
        scores = p_ref[0, :heads].astype(f32)
        for d in range(1, devices):
            scores = scores + p_ref[d, :heads].astype(f32)
        peak = jnp.max(scores, axis=-1, keepdims=True)
        weights = jnp.exp(scores - peak).astype(bf16)
        total = jnp.sum(weights.astype(f32), axis=-1, keepdims=True)
        for d in range(devices):
            w_ref[d] = weights
        lane = lax.broadcasted_iota(jnp.int32, (heads, HEAD_WIDTH), 1)
        head = lax.broadcasted_iota(jnp.int32, (heads, HEAD_WIDTH), 0)
        index = lax.broadcasted_iota(jnp.int32, (8, HEAD_WIDTH), 0)
        tile = jnp.zeros((8, HEAD_WIDTH), f32)
        for at, stat in ((4, peak), (5, total)):
            spread = jnp.zeros((heads, HEAD_WIDTH), f32)
            for n, part in enumerate(thirds(stat)):
                spread = jnp.where(lane == head + n * heads, part, spread)
            tile = jnp.where(index == at, jnp.sum(spread, axis=0, keepdims=True), tile)
        s_ref[...] = tile

    return pl.pallas_call(
        kernel,
        out_shape=(
            jax.ShapeDtypeStruct((devices, heads, length), bf16),
            jax.ShapeDtypeStruct((8, HEAD_WIDTH), f32),
        ),
        compiler_params=SMALL,
        name="fresh_weights",
    )(pieces)


def partial_outputs(weights, states, value_weight, stats, receivers):
    rows, heads, per_row = weights.shape
    features, width = value_weight.shape
    kv_heads = width // HEAD_WIDTH
    group = heads // kv_heads
    local = heads // receivers
    per_kv = group // local

    def kernel(w_ref, x_ref, v_ref, s_ref, o_ref, held):
        row = pl.program_id(0)
        y = jnp.dot(w_ref[0], x_ref[0], preferred_element_type=f32)
        at = pl.multiple_of(row * group, group)
        for j in range(kv_heads):
            held[j, pl.ds(at, group), :] = y[j * group : (j + 1) * group]

        @pl.when(row == rows - 1)
        def _():
            stat = s_ref[...]
            top = lax.broadcasted_iota(jnp.int32, (8, HEAD_WIDTH), 0) < local
            for j in range(kv_heads):
                out = jnp.dot(
                    held[j].astype(bf16),
                    v_ref[:, j * HEAD_WIDTH : (j + 1) * HEAD_WIDTH],
                    preferred_element_type=f32,
                )
                for o in range(rows):
                    tile = out[o * group : (o + 1) * group]
                    for e in range(per_kv):
                        moved = tile if e == 0 else pltpu.roll(tile, group - e * local, 0)
                        o_ref[o * receivers + j * per_kv + e] = jnp.where(top, moved, stat).astype(
                            bf16
                        )

    return pl.pallas_call(
        kernel,
        out_shape=jax.ShapeDtypeStruct((rows * receivers, 8, HEAD_WIDTH), bf16),
        grid=(rows,),
        in_specs=[
            pl.BlockSpec((1, heads, per_row), lambda i: (i, 0, 0)),
            pl.BlockSpec((1, per_row, features), lambda i: (i, 0, 0)),
            pl.BlockSpec((features, width), lambda i: (0, 0)),
            pl.BlockSpec((8, HEAD_WIDTH), lambda i: (0, 0)),
        ],
        out_specs=pl.BlockSpec((rows * receivers, 8, HEAD_WIDTH), lambda i: (0, 0, 0)),
        scratch_shapes=[pltpu.VMEM((kv_heads, rows * group, features), f32)],
        compiler_params=SMALL,
        name="partial_outputs",
    )(weights, in_hbm(states), value_weight, stats)


def cache_attention(pieces, keys, values, limits, start):
    senders, high, length = pieces.shape
    rows, context, width = keys.shape
    local = length // HEAD_WIDTH
    heads = senders * local
    kv_heads = width // HEAD_WIDTH
    group = heads // kv_heads
    per_kv = group // local

    def kernel(limit, first, p_ref, k_ref, v_ref, o_ref, line):
        row = pl.program_id(0)

        @pl.when(row == 0)
        def _():
            for b in range(rows):
                for c in range(local):
                    line[b, pl.ds(c, senders, stride=local), :] = p_ref[
                        :, b, c * HEAD_WIDTH : (c + 1) * HEAD_WIDTH
                    ].astype(f32)

        own = (
            lax.broadcasted_iota(jnp.int32, (heads, width), 1) // HEAD_WIDTH
            == lax.broadcasted_iota(jnp.int32, (heads, width), 0) // group
        )
        q = line[row]
        spread = jnp.where(own, jnp.concatenate([q] * kv_heads, axis=1), 0.0).astype(bf16)
        scores = lax.dot_general(
            spread, k_ref[0], (((1,), (1,)), ((), ())), preferred_element_type=f32
        ) * (1.0 / HEAD_WIDTH**0.5)
        place = lax.broadcasted_iota(jnp.int32, (heads, context), 1) + first[0]
        scores = jnp.where(place < limit[row], scores, masked_score)
        peak = jnp.max(scores, axis=-1, keepdims=True)
        weights = jnp.exp(scores - peak)
        total = jnp.sum(weights, axis=-1, keepdims=True)
        low = lax.broadcasted_iota(jnp.int32, (heads, HEAD_WIDTH), 1) < HALF
        stats = jnp.where(low, peak, total)
        sums = jnp.dot(weights.astype(bf16), v_ref[0], preferred_element_type=f32)
        top = lax.broadcasted_iota(jnp.int32, (group, HEAD_WIDTH), 0) < local
        for j in range(kv_heads):
            tile = sums[j * group : (j + 1) * group, j * HEAD_WIDTH : (j + 1) * HEAD_WIDTH]
            stat = stats[j * group : (j + 1) * group]
            o_ref[j * per_kv, 0] = jnp.where(top, tile, pltpu.roll(stat, local, 0))
            o_ref[j * per_kv + 1, 0] = jnp.where(top, pltpu.roll(tile, local, 0), stat)

    return pl.pallas_call(
        kernel,
        out_shape=jax.ShapeDtypeStruct((senders, rows, group, HEAD_WIDTH), f32),
        grid_spec=pltpu.PrefetchScalarGridSpec(
            num_scalar_prefetch=2,
            grid=(rows,),
            in_specs=[
                pl.BlockSpec((senders, 8, length), lambda i, *_: (0, high // 8 - 1, 0)),
                pl.BlockSpec((1, context, width), lambda i, *_: (i, 0, 0)),
                pl.BlockSpec((1, context, width), lambda i, *_: (i, 0, 0)),
            ],
            out_specs=pl.BlockSpec((senders, 1, group, HEAD_WIDTH), lambda i, *_: (0, i, 0, 0)),
            scratch_shapes=[pltpu.VMEM((rows, heads, HEAD_WIDTH), f32)],
        ),
        compiler_params=SMALL,
        name="cache_attention",
    )(limits, start, pieces, in_hbm(keys), in_hbm(values))


def joined(old, fresh, source, head_at, half, senders):
    devices, rows, group, _ = old.shape
    local = group // 2

    def kernel(source, head_at, old_ref, fresh_ref, o_ref):
        low = lax.broadcasted_iota(jnp.int32, (group, HEAD_WIDTH), 1) < HALF
        lane = lax.broadcasted_iota(jnp.int32, (group, HEAD_WIDTH), 1)
        index = lax.broadcasted_iota(jnp.int32, (group, HEAD_WIDTH), 0)
        chosen = (
            (lax.rem(lane, half) == head_at[0] + index) & (lane < 3 * half) & (index < local)
        )
        for b in range(rows):
            parts = []
            for d in range(devices):
                tile = old_ref[d, b]
                stat = pltpu.roll(tile, local, 0)
                other = swap_halves(stat)
                parts.append((jnp.where(low, stat, other), jnp.where(low, other, stat), tile))
            for n in range(senders):
                at = (b * senders + n) * devices
                tile = fresh_ref[at].astype(f32)
                for d in range(1, devices):
                    tile = tile + fresh_ref[at + d].astype(f32)
                stat = fresh_ref[at + source[0]].astype(f32)
                peak, total = (
                    jnp.sum(
                        jnp.where(chosen, stat[local + k : local + k + 1], 0.0),
                        axis=1,
                        keepdims=True,
                    )
                    for k in range(2)
                )
                parts.append(
                    (
                        jnp.broadcast_to(peak, tile.shape),
                        jnp.broadcast_to(total, tile.shape),
                        tile,
                    )
                )
            top = parts[0][0]
            for peak, _, _ in parts[1:]:
                top = jnp.maximum(top, peak)
            total = jnp.zeros_like(top)
            value = jnp.zeros_like(top)
            for peak, part, tile in parts:
                factor = jnp.exp(peak - top)
                total = total + part * factor
                value = value + tile * factor
            result = value / total
            for c in range(local):
                o_ref[b : b + 1, c * HEAD_WIDTH : (c + 1) * HEAD_WIDTH] = result[c : c + 1]

    return pl.pallas_call(
        kernel,
        out_shape=jax.ShapeDtypeStruct((rows, local * HEAD_WIDTH), f32),
        in_specs=[
            pl.BlockSpec(memory_space=pltpu.SMEM),
            pl.BlockSpec(memory_space=pltpu.SMEM),
            pl.BlockSpec(memory_space=pltpu.VMEM),
            pl.BlockSpec(memory_space=pltpu.VMEM),
        ],
        compiler_params=SMALL,
        name="joined",
    )(source, head_at, old, fresh)


def per_device(
    prefill_states,
    key_weight,
    value_weight,
    page_slot,
    decode_states,
    query_weight,
    cache_keys,
    cache_values,
    cached_length,
):
    tensor_size = lax.axis_size("tensor")
    group_size = lax.axis_size("group")
    tensor_rank = lax.axis_index("tensor")
    group_rank = lax.axis_index("group")
    decode_rows = decode_states.shape[0]
    page_count = page_slot.shape[-1]
    per_owner = page_count // group_size
    block = page_count * PAGE
    fresh_per_row = block // decode_rows
    fresh_length = tensor_size * fresh_per_row
    senders_per_row = group_size // decode_rows
    from_sender = fresh_per_row // senders_per_row
    inv_scale = 1.0 / HEAD_WIDTH**0.5

    local_queries, sent = packed_queries(
        decode_states, query_weight, page_slot, group_size, tensor_size
    )
    local_width = local_queries.shape[1]
    local_heads = local_width // HEAD_WIDTH
    received = exchanged(sent, BOTH)

    first = (group_rank % senders_per_row) * from_sender - fresh_length
    place = (
        jnp.arange(tensor_size, dtype=jnp.int32)[:, None] * fresh_per_row
        + jnp.arange(PAGE, dtype=jnp.int32)[None, :]
        + first
    )
    angles = place[..., None].astype(f32) * FREQUENCY_PAIR
    cosine, sine = jnp.cos(angles), jnp.sin(angles)
    query_position = cached_length + fresh_length
    own_queries = (
        apply_rotary(
            local_queries.reshape(decode_rows, local_heads, HEAD_WIDTH), query_position[:, None]
        )
        .reshape(decode_rows, local_width)
        .astype(bf16)
    )
    keys = partial_keys(in_hbm(prefill_states), key_weight, cosine, sine)

    head_total = tensor_size * local_heads
    order = lax.dynamic_slice(
        received, (group_rank * tensor_size, local_heads, 0), (tensor_size, 1, page_count)
    )
    order = order.reshape(tensor_size, page_count).astype(jnp.int32)
    turn = np.arange(per_owner)[:, None] * PAGE * np.concatenate([FREQUENCY, FREQUENCY])[None]
    tables = (np.stack([np.cos(turn), np.sin(turn)]) * inv_scale).astype(np.float32)
    scores = partial_scores(order, keys, received, own_queries, jnp.asarray(tables), group_size)
    half = head_total * group_size // tensor_size
    fresh_row = scores.shape[-1]
    pieces = exchanged(scores, "tensor")

    states = sorted_states(order, prefill_states, group_size, per_owner)

    weights, stats = fresh_weights(pieces, half)
    weights = exchanged(weights, "tensor")

    context_dev = cache_keys.shape[1]
    start = (tensor_rank * context_dev).astype(jnp.int32).reshape(1)
    old = cache_attention(pieces, cache_keys, cache_values, cached_length, start)
    old = exchanged(old, "tensor")

    weights = weights.reshape(group_size, head_total, fresh_row)
    outputs = partial_outputs(weights, states, value_weight, stats, tensor_size)
    outputs = exchanged(outputs, BOTH)

    per_source = half // local_heads
    source = group_rank * (tensor_size // group_size) + tensor_rank // per_source
    head_at = (tensor_rank % per_source) * local_heads
    result = joined(
        old,
        outputs,
        source.astype(jnp.int32).reshape(1),
        head_at.astype(jnp.int32).reshape(1),
        half,
        senders_per_row,
    )
    return result.astype(bf16)


def solution(mesh):
    placed = (
        P("group", "tensor"),
        P("tensor", None),
        P("tensor", None),
        P("group", "tensor", None),
        P("group", None),
        P(None, "tensor"),
        P("group", "tensor", None),
        P("group", "tensor", None),
        P("group"),
    )

    return jax.shard_map(
        per_device, mesh=mesh, in_specs=placed, out_specs=P("group", "tensor"), check_vma=False
    )
```

time: 140 us -> 124 us (0.89)
  blocking collectives: 0 us -> 20.7 us
  waiting for transfers between devices: 35.3 us -> 15.6 us
  matrix products: 11 us -> 0 us
  starting transfers between devices: 35.9 us -> 29.5 us
  Pallas kernels: 41.6 us -> 46.9 us
  other arithmetic: 4.25 us -> 1.27 us
    all_to_all x0 -> x1, blocking collectives: none -> 20.7 us  [exchanged(): return lax.all_to_all(x, axis, 0, 0, tiled=True)]
    all_to_all x6 -> x4, waiting for transfers between devices: 35.3 us -> 15.6 us  [exchanged(): return lax.all_to_all(x, axis, 0, 0, tiled=True)]
    dot_general x3 -> x0, matrix products: 11 us -> none  [the longest x1 4.56 us: per_device(): jnp.dot(decode_states, query_weight, preferred_element_type=f32)]
    all_to_all x6 -> x4, starting transfers between devices: 35.9 us -> 29.5 us  [exchanged(): return lax.all_to_all(x, axis, 0, 0, tiled=True)]
    pallas_call x4 -> x7, Pallas kernels: 34.7 us -> 40.5 us  [the longest x1 12.4 us: partial_keys(): pl.pallas_call(kernel, out_shape=pltpu.VMEM((tokens, width), bf16), grid=...]
    unnamed x23 -> x21, local copies, waits for them, and re-layouts: 2.97 us -> 8.23 us
    all_to_all x2 -> x0, local copies, waits for them, and re-layouts: 2.53 us -> none  [the longest x1 2.02 us: per_device(): outputs = lax.all_to_all(outputs, BOTH, 0, 0, tiled=True)]
  transfers between devices with their start and end apart: 6 -> 4, of which waited for: 5 -> 2; matrix products, arithmetic and copies ran while one was open for 9% -> 1% of each run, Pallas kernels for 18% -> 27%
where the time goes in v2:
time: 124 us; the launch traced here: 122 us
  Pallas kernels  46.9 us (38%)
  starting transfers between devices  29.5 us (24%)
  blocking collectives  20.7 us (17%)
  waiting for transfers between devices  15.6 us (13%)
  local copies, waits for them, and re-layouts  8.27 us (7%)
  other arithmetic  1.27 us (1%)
    all_to_all x4, starting transfers between devices, exchanged(): return lax.all_to_all(x, axis, 0, 0, tiled=True)  29.5 us
    all_to_all x1, blocking collectives, exchanged(): return lax.all_to_all(x, axis, 0, 0, tiled=True)  20.7 us
    all_to_all x4, waiting for transfers between devices, exchanged(): return lax.all_to_all(x, axis, 0, 0, tiled=True)  15.6 us
    pallas_call x1, Pallas kernels, partial_keys(): pl.pallas_call(kernel, out_shape=pltpu.VMEM((tokens, width), bf16), grid=...  12.4 us
    unnamed x21, local copies, waits for them, and re-layouts  8.23 us
    pallas_call x1, Pallas kernels, sorted_states(): pl.pallas_call(kernel, out_shape=pltpu.HBM((rows, per_row, features), bf1...  7.5 us
    pallas_call x1, Pallas kernels, packed_queries(): pl.pallas_call(kernel, out_shape=(jax.ShapeDtypeStruct((rows, width), f32...  7.29 us
    pallas_call x1, Pallas kernels, cache_attention(): pl.pallas_call(kernel, out_shape=jax.ShapeDtypeStruct((senders, rows, gro...  6.97 us
  transfers between devices with their start and end apart: 4, of which 2 were waited for; matrix products, arithmetic and copies ran while one was open for 1% of the time, Pallas kernels for 27%

profile of v2, /device:TPU:1, one launch (start us, length us, event | category | flops | bytes accessed | tf_op | source)
XLA Modules:
  0.0 122.5 jit_solution(11842042587423990342)
XLA Ops:
  0.0 0.9 copy-done.4
  0.9 0.7 copy-done.6
  1.6 7.3 %packed_queries.1 = (f32[4,512]{1,0:T(4,128)S(1)}, bf16[128,8,128]{2,1,0:T(8,128)(2,1)}) custom-call(bf16[4,8192]{1,0:T(4,128)(2,1)S(1)} %copy-done.4, bf16[8192,512]{1,0:T(8,128)(2,1)} %w_ref.2, s32[1,1,32]{2,1,0:T(1,128)S(1)} %copy-done.6), custom_call_target="tpu_custom_call" | custom-call | tf_op jit(solution)/shard_map/packed_queries/pallas_call | solution.py:96
  8.9 11.5 %all-to-all-start = ((bf16[128,8,128]{2,1,0:T(8,128)(2,1)}), bf16[128,8,128]{2,1,0:T(8,128)(2,1)S(1)}, u32[]{:S(2)}, u32[]{:S(2)}) async-start(bf16[128,8,128]{2,1,0:T(8,128)(2,1)} %get-tuple-element.9), calls=%async_computation | async-start | bytes 524288 | tf_op jit(solution)/shard_map/all_to_all | solution.py:49
  20.5 0.1 multiply_cosine_fusion.1
  20.6 0.1 subtract_convert_fusion
  20.7 0.1 maximum_bitcast_fusion
  20.8 0.3 multiply_sine_fusion
  21.2 12.4 %partial_keys.1 = bf16[4096,1024]{1,0:T(8,128)(2,1)S(1)} custom-call(bf16[4096,512]{1,0:T(8,128)(2,1)} %x_ref.1, bf16[512,1024]{1,0:T(8,128)(2,1)S(1)} %copy-done.3, f32[16,8,128]{2,1,0:T(8,128)S(1)} %get-tuple-element.16.c_ref, f32[16,8,128]{2,1,0:T(8,128)S(1)} %get-tuple-element.15.s_ref), custom_call_target="tpu_custom_call" | custom-call | tf_op jit(solution)/shard_map/partial_keys/pallas_call | solution.py:150
  33.6 3.2 %copy-done = bf16[4096,1024]{1,0:T(8,128)(2,1)} copy-done((bf16[4096,1024]{1,0:T(8,128)(2,1)}, bf16[4096,1024]{1,0:T(8,128)(2,1)S(1)}, u32[]{:S(2)}) %copy-start) | copy-done | bytes 8388632
  36.9 3.4 %copy-done.1 = bf16[4096,1024]{1,0:T(8,128)(2,1)S(1)} copy-done((bf16[4096,1024]{1,0:T(8,128)(2,1)S(1)}, bf16[4096,1024]{1,0:T(8,128)(2,1)}, u32[]{:S(2)}) %copy-start.1) | copy-done | bytes 8388632
  40.2 5.1 %partial_scores.1 = bf16[16,40,512]{2,1,0:T(8,128)(2,1)S(1)} custom-call(s32[16,32]{1,0:T(8,128)S(1)} %fusion.order, bf16[512,8,1024]{2,1,0:T(8,128)(2,1)S(1)} %bitcast.16, bf16[128,8,128]{2,1,0:T(8,128)(2,1)S(1)} %all-to-all-done.r_ref, bf16[8,512]{1,0:T(8,128)(2,1)S(1)} %pad.4.own_ref, f32[2,4,128]{2,1,0:T(4,128)S(1)} %copy-done.5), custom_call_target="tpu_custom_call" | custom-call | tf_op jit(solution)/shard_map/partial_scores/pallas_call | solution.py:228
  45.3 20.7 %all_to_all.25.p_ref = bf16[16,40,512]{2,1,0:T(8,128)(2,1)S(1)} all-to-all(bf16[16,40,512]{2,1,0:T(8,128)(2,1)S(1)} %partial_scores.1), channel_id=1, replica_groups=mesh['group'=8,'tensor'=16] {'tensor'}, dimensions={0} | all-to-all | bytes 1310720 | tf_op jit(solution)/shard_map/all_to_all | solution.py:49
  66.0 1.0 fresh_weights.1
  67.0 4.0 %all-to-all-start.3 = ((bf16[16,32,512]{2,1,0:T(8,128)(2,1)}), bf16[16,32,512]{2,1,0:T(8,128)(2,1)S(1)}, u32[]{:S(2)}, u32[]{:S(2)}) async-start(bf16[16,32,512]{2,1,0:T(8,128)(2,1)} %get-tuple-element.11), calls=%async_computation.3 | async-start | bytes 1048576 | tf_op jit(solution)/shard_map/all_to_all | solution.py:49
  71.0 7.0 %cache_attention.1 = f32[16,4,8,128]{3,2,1,0:T(8,128)} custom-call(s32[4]{0:T(128)S(1)} %copy-done.7, s32[1]{0:T(128)} %bitcast.2.first, bf16[16,40,512]{2,1,0:T(8,128)(2,1)S(1)} %all_to_all.25.p_ref, bf16[4,512,1024]{2,1,0:T(8,128)(2,1)} %k_ref.1, bf16[4,512,1024]{2,1,0:T(8,128)(2,1)} %v_ref.2), custom_call_target="tpu_custom_call" | custom-call | tf_op jit(solution)/shard_map/cache_attention/pallas_call | solution.py:426
  78.0 4.3 %all-to-all-done.3 = bf16[16,32,512]{2,1,0:T(8,128)(2,1)S(1)} async-done(((bf16[16,32,512]{2,1,0:T(8,128)(2,1)}), bf16[16,32,512]{2,1,0:T(8,128)(2,1)S(1)}, u32[]{:S(2)}, u32[]{:S(2)}) %all-to-all-start.3) | async-done | bytes 524320 | tf_op jit(solution)/shard_map/all_to_all | solution.py:49
  82.3 4.6 %all-to-all-start.2 = ((f32[16,4,8,128]{3,2,1,0:T(8,128)}), f32[16,4,8,128]{3,2,1,0:T(8,128)S(1)}, u32[]{:S(2)}, u32[]{:S(2)}) async-start(f32[16,4,8,128]{3,2,1,0:T(8,128)} %cache_attention.1), calls=%async_computation.2 | async-start | bytes 524288 | tf_op jit(solution)/shard_map/all_to_all | solution.py:49
  86.9 7.5 %sorted_states.1.x_ref = bf16[8,512,512]{2,1,0:T(8,128)(2,1)} custom-call(s32[16,32]{1,0:T(8,128)S(1)} %fusion.order, bf16[512,8,512]{2,1,0:T(8,128)(2,1)} %bitcast.18), custom_call_target="tpu_custom_call" | custom-call | tf_op jit(solution)/shard_map/sorted_states/pallas_call | solution.py:273
  94.4 6.4 %partial_outputs.1 = bf16[128,8,128]{2,1,0:T(8,128)(2,1)} custom-call(bf16[8,64,512]{2,1,0:T(8,128)(2,1)S(1)} %bitcast.17, bf16[8,512,512]{2,1,0:T(8,128)(2,1)} %sorted_states.1.x_ref, bf16[512,1024]{1,0:T(8,128)(2,1)S(1)} %copy-done.2, f32[8,128]{1,0:T(8,128)S(1)} %get-tuple-element.12.s_ref), custom_call_target="tpu_custom_call" | custom-call | tf_op jit(solution)/shard_map/partial_outputs/pallas_call | solution.py:365
  100.8 9.4 %all-to-all-start.4 = ((bf16[128,8,128]{2,1,0:T(8,128)(2,1)}), bf16[128,8,128]{2,1,0:T(8,128)(2,1)S(1)}, u32[]{:S(2)}, u32[]{:S(2)}) async-start(bf16[128,8,128]{2,1,0:T(8,128)(2,1)} %partial_outputs.1), calls=%async_computation.4 | async-start | bytes 524288 | tf_op jit(solution)/shard_map/all_to_all | solution.py:49
  110.3 11.3 %all-to-all-done.4.fresh_ref = bf16[128,8,128]{2,1,0:T(8,128)(2,1)S(1)} async-done(((bf16[128,8,128]{2,1,0:T(8,128)(2,1)}), bf16[128,8,128]{2,1,0:T(8,128)(2,1)S(1)}, u32[]{:S(2)}, u32[]{:S(2)}) %all-to-all-start.4) | async-done | bytes 262176 | tf_op jit(solution)/shard_map/all_to_all | solution.py:49
  121.6 0.3 joined.1
  121.9 0.6 convert_element_type.31
  (26 shorter events, 0.2 us)
Async XLA Ops:
  0.0 20.5 %copy-start.9 = (f32[64]{0:T(128)S(1)}, f32[64]{0:T(128)}, u32[]{:S(2)}) copy-start(f32[64]{0:T(128)} %constant.71.clone) | copy-start | bytes 772
  0.0 20.8 %copy-start.8 = (f32[128]{0:T(128)S(1)}, f32[128]{0:T(128)}, u32[]{:S(2)}) copy-start(f32[128]{0:T(128)} %constant.70.clone) | copy-start | bytes 1540
  0.0 21.1 %copy-start.3 = (bf16[512,1024]{1,0:T(8,128)(2,1)S(1)}, bf16[512,1024]{1,0:T(8,128)(2,1)}, u32[]{:S(2)}) copy-start(bf16[512,1024]{1,0:T(8,128)(2,1)} %w_ref.3) | copy-start | bytes 3145732
  0.0 0.9 copy-start.4
  0.9 0.7 copy-start.6
  1.6 18.8 %copy-start.7 = (s32[4]{0:T(128)S(1)}, s32[4]{0:T(128)}, u32[]{:S(2)}) copy-start(s32[4]{0:T(128)} %limit.1) | copy-start | bytes 52
  8.9 27.9 %all-to-all-start = ((bf16[128,8,128]{2,1,0:T(8,128)(2,1)}), bf16[128,8,128]{2,1,0:T(8,128)(2,1)S(1)}, u32[]{:S(2)}, u32[]{:S(2)}) async-start(bf16[128,8,128]{2,1,0:T(8,128)(2,1)} %get-tuple-element.9), calls=%async_computation | async-start | bytes 524288 | tf_op jit(solution)/shard_map/all_to_all | solution.py:49
  21.1 15.7 %copy-start.5 = (f32[2,4,128]{2,1,0:T(4,128)S(1)}, f32[2,4,128]{2,1,0:T(4,128)}, u32[]{:S(2)}) copy-start(f32[2,4,128]{2,1,0:T(4,128)} %constant.72.clone.t_ref) | copy-start | bytes 12292
  33.5 3.3 %copy-start = (bf16[4096,1024]{1,0:T(8,128)(2,1)}, bf16[4096,1024]{1,0:T(8,128)(2,1)S(1)}, u32[]{:S(2)}) copy-start(bf16[4096,1024]{1,0:T(8,128)(2,1)S(1)} %partial_keys.1) | copy-start | bytes 25165828
  36.8 3.4 %copy-start.1 = (bf16[4096,1024]{1,0:T(8,128)(2,1)S(1)}, bf16[4096,1024]{1,0:T(8,128)(2,1)}, u32[]{:S(2)}) copy-start(bf16[4096,1024]{1,0:T(8,128)(2,1)} %copy-done) | copy-start | bytes 25165828
  67.0 15.3 %all-to-all-start.3 = ((bf16[16,32,512]{2,1,0:T(8,128)(2,1)}), bf16[16,32,512]{2,1,0:T(8,128)(2,1)S(1)}, u32[]{:S(2)}, u32[]{:S(2)}) async-start(bf16[16,32,512]{2,1,0:T(8,128)(2,1)} %get-tuple-element.11), calls=%async_computation.3 | async-start | bytes 1048576 | tf_op jit(solution)/shard_map/all_to_all | solution.py:49
  82.3 18.6 %all-to-all-start.2 = ((f32[16,4,8,128]{3,2,1,0:T(8,128)}), f32[16,4,8,128]{3,2,1,0:T(8,128)S(1)}, u32[]{:S(2)}, u32[]{:S(2)}) async-start(f32[16,4,8,128]{3,2,1,0:T(8,128)} %cache_attention.1), calls=%async_computation.2 | async-start | bytes 524288 | tf_op jit(solution)/shard_map/all_to_all | solution.py:49
  86.9 7.5 %copy-start.2 = (bf16[512,1024]{1,0:T(8,128)(2,1)S(1)}, bf16[512,1024]{1,0:T(8,128)(2,1)}, u32[]{:S(2)}) copy-start(bf16[512,1024]{1,0:T(8,128)(2,1)} %v_ref.3) | copy-start | bytes 3145732
  100.8 20.8 %all-to-all-start.4 = ((bf16[128,8,128]{2,1,0:T(8,128)(2,1)}), bf16[128,8,128]{2,1,0:T(8,128)(2,1)S(1)}, u32[]{:S(2)}, u32[]{:S(2)}) async-start(bf16[128,8,128]{2,1,0:T(8,128)(2,1)} %partial_outputs.1), calls=%async_computation.4 | async-start | bytes 524288 | tf_op jit(solution)/shard_map/all_to_all | solution.py:49
